TPU v7x, 512 devices: a whole 4x8x8 slice. The times are simulated.
512 devices in a mesh: rep: 4 (over y_hi, core), sp: 128 (over y_lo, z, x).
Axes of the slice: x: 4, y: 8 (y_hi: 2, y_lo: 4; y = y_hi * 4 + y_lo), z: 8, core: 2. Of those that a mesh axis runs over, the one named last changes fastest.
Arguments:
- film_start: float32 [4, 2048, 2048], P('rep', 'sp'), may hold values from 0.2 to 2
- evaporation: float32 [4, 2048, 2048], P('rep', 'sp'), may hold values from 0.05 to 0.5
- contact_mask: int32 [4, 2048, 2048], P('rep', 'sp'), may hold values 0 or 1
- first_classes: int32 [4, 2048, 16], P('rep'), may hold values from 0 to 3
- second_classes: int32 [4, 2048, 16], P('rep', 'sp'), may hold values from 0 to 3
- span_inverses: float32 [4, 128, 128], replicated, may hold values from -0.4 to 1
- conv_weight: bfloat16 [3, 3, 4, 64], replicated, may hold values from -0.5 to 0.5
- mixing_weight: bfloat16 [64, 64], replicated, may hold values from -0.75 to 0.75
- flux_weight: bfloat16 [64], replicated, may hold values from -0.75 to 0.75
- film_cotangent: float32 [4, 2048, 2048], P('rep', 'sp'), may hold values from -6 to 6
Outputs:
- final_film: float32 [4, 2048, 2048], P('rep', 'sp')
- film_grad: float32 [4, 2048, 2048], P('rep', 'sp')
- conv_grad: float32 [3, 3, 4, 64], replicated
- mixing_grad: float32 [64, 64], replicated
- flux_grad: float32 [64], replicated
All inputs are finite; a program needn't handle non-finite values. No bound on the sum of `contact_mask` on one device may be relied on, other than what follows from the above.
Results may differ from a plain program's by a relative error of at most 0.019.
Values may be sent and summed in bfloat16 or wider, within the bound.
A program may use at most 128 MiB of HBM per device.

v0:
```python
from functools import partial
import math

import jax
import jax.numpy as jnp
from jax import lax
from jax.sharding import PartitionSpec as P

STEPS = 1


time_step = 0.5


def extended(array, sides, width):
    for axis, dim in sides:
        size, length = (lax.axis_size(axis), array.shape[dim])
        up = [(i, (i + 1) % size) for i in range(size - 1)]
        down = [(j, i) for i, j in up]
        last = lax.slice_in_dim(array, length - width, length, axis=dim)
        first = lax.slice_in_dim(array, 0, width, axis=dim)
        before = lax.ppermute(last, axis, up)
        after = lax.ppermute(first, axis, down)
        array = jnp.concatenate([before, array, after], axis=dim)
    return array


def select_product(tile_rows, matrix, hits, current):
    product = jnp.dot(tile_rows, matrix, precision=lax.Precision.HIGHEST)
    return jnp.where(hits[:, None], product, current)


def keep_same(current):
    return current


def apply_spans(vectors, classes, inverses, transpose):
    count = vectors.shape[0]
    tile_size = math.gcd(128, count)
    line_order = jnp.argsort(classes, stable=True)
    ordered = jnp.take(vectors, line_order, axis=0)
    ordered_cls = jnp.take(classes, line_order)
    results = []
    for start in range(0, count, tile_size):
        tile_rows = ordered[start : start + tile_size]
        tile_cls = ordered_cls[start : start + tile_size]
        result = jnp.zeros_like(tile_rows)
        for group in range(inverses.shape[0]):
            matrix = inverses[group] if transpose else inverses[group].T
            hits = tile_cls == group
            result = lax.cond(
                jnp.any(hits), partial(select_product, tile_rows, matrix, hits), keep_same, result
            )
        results.append(result)
    joined = jnp.concatenate(results, axis=0)
    return jnp.zeros_like(vectors).at[line_order].set(joined)


def solve_lines(lines, classes, inverses, transpose):
    span = inverses.shape[1]
    vectors = lines.reshape(-1, span)
    return apply_spans(vectors, classes.reshape(-1), inverses, transpose).reshape(lines.shape)


def relayout(field):
    moved = lax.all_to_all(field, "sp", split_axis=2, concat_axis=1, tiled=True)
    return jnp.swapaxes(moved, 1, 2)


def split_columns(padded, width):
    count = (padded.shape[-1] - 2) // width
    return jnp.stack(
        [padded[..., number * width : number * width + width + 2] for number in range(count)]
    )


def join_blocks(blocks):
    moved = jnp.moveaxis(blocks, 0, -2)
    return moved.reshape(moved.shape[:-2] + (moved.shape[-2] * moved.shape[-1],))


def cut_blocks(field, width):
    shape = field.shape
    reshaped = field.reshape(shape[:-1] + (shape[-1] // width, width))
    return jnp.moveaxis(reshaped, -2, 0)


def join_padded(blocks):
    middle = jnp.moveaxis(blocks[..., 1:-1], 0, -2)
    left = jnp.moveaxis(blocks[..., 0], 0, -1)
    right = jnp.moveaxis(blocks[..., -1], 0, -1)
    middle = middle.at[..., :-1, -1].add(left[..., 1:])
    middle = middle.at[..., 1:, 0].add(right[..., :-1])
    return middle.reshape(middle.shape[:-2] + (middle.shape[-2] * middle.shape[-1],))


def tap_stack(piece):
    rows = piece.shape[2] - 2
    cols = piece.shape[3] - 2
    return jnp.concatenate(
        [
            piece[:, :, row_tap : row_tap + rows, col_tap : col_tap + cols]
            for row_tap in range(3)
            for col_tap in range(3)
        ],
        axis=0,
    )


def closure_forward(piece, conv_w, mixing_w, flux_w):
    stacked = tap_stack(piece)
    conv_matrix = conv_w.reshape(-1, conv_w.shape[-1])
    first_tanh = jnp.tanh(
        jnp.einsum("ko,krxy->orxy", conv_matrix, stacked, preferred_element_type=jnp.float32)
    )
    first_act = first_tanh.astype(jnp.bfloat16)
    second_tanh = jnp.tanh(
        jnp.einsum("op,orxy->prxy", mixing_w, first_act, preferred_element_type=jnp.float32)
    )
    second_act = second_tanh.astype(jnp.bfloat16)
    flux = jnp.einsum("p,prxy->rxy", flux_w, second_act, preferred_element_type=jnp.float32)
    return (flux, first_tanh, first_act, second_tanh, second_act, stacked)


def closure_backward(piece, flux_cot, conv_w, mixing_w, flux_w):
    rows = piece.shape[2] - 2
    cols = piece.shape[3] - 2
    channels = piece.shape[0]
    flux, first_tanh, first_act, second_tanh, second_act, stacked = closure_forward(
        piece, conv_w, mixing_w, flux_w
    )
    flux_part = jnp.einsum("prxy,rxy->p", second_act, flux_cot, preferred_element_type=jnp.float32)
    second_cot = (flux_w.astype(jnp.float32)[:, None, None, None] * flux_cot[None]).astype(
        jnp.bfloat16
    )
    pre_second_cot = second_cot * (1.0 - second_tanh * second_tanh)
    mixing_part = jnp.einsum(
        "orxy,prxy->op", first_act, pre_second_cot, preferred_element_type=jnp.float32
    )
    first_cot = jnp.einsum(
        "op,prxy->orxy", mixing_w, pre_second_cot, preferred_element_type=jnp.float32
    ).astype(jnp.bfloat16)
    pre_first_cot = first_cot * (1.0 - first_tanh * first_tanh)
    conv_part = jnp.einsum(
        "orxy,krxy->ko", pre_first_cot, stacked, preferred_element_type=jnp.float32
    ).reshape(conv_w.shape)
    conv_matrix = conv_w.reshape(-1, conv_w.shape[-1])
    tap_cots = jnp.einsum(
        "ko,orxy->krxy", conv_matrix, pre_first_cot, preferred_element_type=jnp.float32
    )
    piece_cot = jnp.zeros(piece.shape, jnp.float32)
    for row_tap in range(3):
        for col_tap in range(3):
            number = row_tap * 3 + col_tap
            term = tap_cots[number * channels : (number + 1) * channels]
            piece_cot = piece_cot.at[:, :, row_tap : row_tap + rows, col_tap : col_tap + cols].add(
                term
            )
    edges = jnp.stack([pre_first_cot[:, :, 0], pre_first_cot[:, :, -1]], axis=2)
    return (piece_cot, conv_part, mixing_part, flux_part, edges)


def rim_terms(neighbour, conv_w, row_tap, cols):
    padded = jnp.pad(neighbour, ((0, 0), (0, 0), (1, 1)))
    total = None
    for col_tap in range(3):
        term = jnp.einsum(
            "co,ory->cry",
            conv_w[row_tap, col_tap],
            padded[:, :, 2 - col_tap : 2 - col_tap + cols],
            preferred_element_type=jnp.float32,
        )
        total = term if total is None else total + term
    return total


def on_device(
    film_start,
    evaporation,
    contact_mask,
    first_classes,
    second_classes,
    span_inverses,
    conv_weight,
    mixing_weight,
    flux_weight,
    film_cotangent,
):
    maskf = contact_mask.astype(jnp.float32)
    side = film_start.shape[2]
    side_dev = film_start.shape[1]
    nspan = first_classes.shape[2]
    sp_index = lax.axis_index("sp")
    block_width = min(512, side)

    def first_solve(field, transpose):
        own_first = lax.dynamic_slice(
            first_classes, (0, sp_index * side_dev, 0), (1, side_dev, nspan)
        )
        solved = solve_lines(relayout(field), own_first, span_inverses, transpose)
        return relayout(solved)

    def forward_block(piece):
        return closure_forward(piece, conv_weight, mixing_weight, flux_weight)[0]

    def backward_block(items):
        return closure_backward(items[0], items[1], conv_weight, mixing_weight, flux_weight)

    height = film_start
    step = 0
    features = jnp.stack([height, height * height, maskf, evaporation]).astype(jnp.bfloat16)
    rimmed = extended(features, (("sp", 2),), 1)
    padded = jnp.pad(rimmed, ((0, 0), (0, 0), (0, 0), (1, 1)))
    pieces = split_columns(padded, block_width)
    flux = join_blocks(lax.map(forward_block, pieces))
    source_side = height + time_step * (flux - maskf * evaporation)
    across = first_solve(source_side, False)
    saved = [(height, pieces)]
    height = solve_lines(across, second_classes, span_inverses, False)
    final_film = height
    grad = film_cotangent
    conv_total = jnp.zeros(conv_weight.shape, jnp.float32)
    mixing_total = jnp.zeros(mixing_weight.shape, jnp.float32)
    flux_total = jnp.zeros(flux_weight.shape, jnp.float32)
    for step in reversed(range(STEPS)):
        height, pieces = saved[step]
        back = solve_lines(grad, second_classes, span_inverses, True)
        source_grad = first_solve(back, True)
        flux_cot = cut_blocks(time_step * source_grad, block_width)
        piece_cots, conv_parts, mixing_parts, flux_parts, edges = lax.map(
            backward_block, (pieces, flux_cot)
        )
        conv_total = jnp.sum(conv_parts, axis=0)
        mixing_total = jnp.sum(mixing_parts, axis=0)
        flux_total = jnp.sum(flux_parts, axis=0)
        whole = join_padded(piece_cots)
        inner = whole[:, :, 1:-1]
        rims = extended(join_blocks(edges).astype(jnp.bfloat16), (("sp", 2),), 1).astype(
            jnp.float32
        )
        inner = inner.at[:, :, 0].add(rim_terms(rims[:, :, 0], conv_weight, 2, side))
        inner = inner.at[:, :, -1].add(rim_terms(rims[:, :, 3], conv_weight, 0, side))
        feature_cot = inner.astype(jnp.bfloat16)
        grad = source_grad + feature_cot[0] + 2.0 * height * feature_cot[1]
    conv_sum, mixing_sum, flux_sum = lax.psum((conv_total, mixing_total, flux_total), ("rep", "sp"))
    scale = 1.0 / math.sqrt(lax.axis_size("rep") * film_start.shape[0] * side * side)
    return (final_film, grad, conv_sum * scale, mixing_sum * scale, flux_sum * scale)


def solution(mesh):
    return jax.shard_map(
        on_device,
        mesh=mesh,
        in_specs=(
            P("rep", "sp", None),
            P("rep", "sp", None),
            P("rep", "sp", None),
            P("rep", None, None),
            P("rep", "sp", None),
            P(),
            P(),
            P(),
            P(),
            P("rep", "sp", None),
        ),
        out_specs=(P("rep", "sp", None), P("rep", "sp", None), P(), P(), P()),
        check_vma=False,
    )
```

profile of v0, /device:TPU:1, one launch (start us, length us, event | category | flops | bytes accessed | tf_op | source)
XLA Modules:
  0.0 486.8 jit_solution(13716353377885899539)
XLA Ops:
  3.0 3.9 collective-permute-start
  9.2 3.2 sort.35
  12.4 3.2 sort.36
  31.3 9.3 %reduce.65 = f32[2048,16]{1,0:T(8,128)S(1)} reduce(f32[2048,1,16]{2,1,0:T(1,128)S(1)} %bitcast.494, f32[]{:T(128)} %broadcast.556), dimensions={1}, to_apply=%bitcast.318.reduce_sub_computation | reduce | bytes 262148
  41.7 19.8 %all-to-all-start.2 = ((f32[128,1,256]{2,1,0:T(1,128)}), f32[128,1,256]{2,1,0:T(1,128)S(1)}, u32[]{:S(2)}, u32[]{:S(2)}) async-start(f32[128,1,256]{2,1,0:T(1,128)} %reshape.1187), calls=%async_computation.2 | async-start | bytes 262144 | tf_op jit(solution)/shard_map/all_to_all | solution.py:66
  82.6 9.3 %reduce.67 = f32[2048,16]{1,0:T(8,128)S(1)} reduce(f32[2048,1,16]{2,1,0:T(1,128)S(1)} %bitcast.495, f32[]{:T(128)} %broadcast.556), dimensions={1}, to_apply=%bitcast.320.reduce_sub_computation | reduce | bytes 262148
  93.0 13.2 %all-to-all-start.3 = ((f32[128,1,256]{2,1,0:T(1,128)}), f32[128,1,256]{2,1,0:T(1,128)S(1)}, u32[]{:S(2)}, u32[]{:S(2)}) async-start(f32[128,1,256]{2,1,0:T(1,128)} %reshape.1189), calls=%async_computation.3 | async-start | bytes 262144 | tf_op jit(solution)/shard_map/all_to_all | solution.py:66
  106.3 7.4 %while.44 = (s32[]{:T(128)}, f32[4,1,16,512]{3,2,1,0:T(8,128)S(1)}, bf16[4,4,1,18,514]{4,1,3,2,0:T(4,128)(2,1)S(1)}, bf16[3,3,4,64]{3,2,1,0:T(4,128)(2,1)S(1)}, ...) while((s32[]{:T(128)}, f32[4,1,16,512]{3,2,1,0:T(8,128)S(1)}, ...), condition=%wide.region_11.13_spmd, body=%wide.region_10.12_spmd.sunk | while | flops 106954752 | bytes 5314845 | solution.py:215
  124.0 156.3 %while.45 = (s32[]{:T(128)}, f32[4,4,1,18,514]{4,1,3,2,0:T(4,128)}, f32[4,3,3,4,64]{4,3,2,1,0:T(4,128)}, f32[4,64,64]{2,1,0:T(8,128)}, f32[4,64]{1,0:T(4,128)}, ...) while((s32[]{:T(128)}, f32[4,4,1,18,514]{4,1,3,2,0:T(4,128)}, ...), condition=%wide.region_90.93_spmd, body=%wide.region_88.92_spmd.sunk | while | flops 327188544 | bytes 51537856 | solution.py:230
  132.5 3.1 fusion.288
  140.6 4.0 scatter-add.90
  146.7 4.0 scatter-add.91
  150.9 2.8 scatter-add.92
  156.8 2.8 scatter-add.94
  171.6 3.1 fusion.288
  179.7 4.0 scatter-add.90
  185.7 4.0 scatter-add.91
  210.6 3.1 fusion.288
  218.7 4.0 scatter-add.90
  224.7 4.0 scatter-add.91
  249.6 3.1 fusion.288
  257.7 4.0 scatter-add.90
  263.7 4.0 scatter-add.91
  280.3 4.8 copy.228
  285.7 5.3 %fusion.141 = (f32[4,4,1,18,512]{3,1,0,4,2:T(4,128)S(1)}, f32[4,1,18,4,512]{2,0,3,4,1:T(4,128)}) fusion(f32[4,4,1,18,514]{3,1,0,4,2:T(4,128)} %copy.228), kind=kLoop, calls=%fused_computation.279 | loop fusion | bytes 1769472 | tf_op jit(solution)/shard_map/slice | solution.py:89
  299.7 4.3 copy.231
  307.4 9.3 %reduce.69 = f32[2048,16]{1,0:T(8,128)S(1)} reduce(f32[2048,1,16]{2,1,0:T(1,128)S(1)} %bitcast.496, f32[]{:T(128)} %broadcast.556), dimensions={1}, to_apply=%bitcast.314.reduce_sub_computation | reduce | bytes 262148
  317.8 15.1 %all-to-all-start = ((f32[128,1,256]{2,1,0:T(1,128)}), f32[128,1,256]{2,1,0:T(1,128)S(1)}, u32[]{:S(2)}, u32[]{:S(2)}) async-start(f32[128,1,256]{2,1,0:T(1,128)} %reshape.1183), calls=%async_computation | async-start | bytes 262144 | tf_op jit(solution)/shard_map/all_to_all | solution.py:66
  333.0 100.6 %all-reduce.4 = (f32[3,3,4,64]{3,2,1,0:T(4,128)S(1)}, f32[64,64]{1,0:T(8,128)S(1)}, f32[64]{0:T(128)S(1)}) all-reduce(f32[3,3,4,64]{3,2,1,0:T(4,128)S(1)} %reduce_sum.27, f32[64,64]{1,0:T(8,128)S(1)} %reduce_sum.28, f32[64]{0:T(128)S(1)} %reduce_sum.29), channel_id=1, replica_groups=mesh['rep'=4,'sp'=128] {'rep','sp'}, use_global_device_ids=true, to_apply=%region_93.96 | all-reduce | flops 6464 | bytes 51712 | tf_op jit(solution)/shard_map/psum | solution.py:245
  444.1 9.3 %reduce.71 = f32[2048,16]{1,0:T(8,128)S(1)} reduce(f32[2048,1,16]{2,1,0:T(1,128)S(1)} %bitcast.497, f32[]{:T(128)} %broadcast.556), dimensions={1}, to_apply=%bitcast.316.reduce_sub_computation | reduce | bytes 262148
  454.5 8.7 %all-to-all-start.1 = ((f32[128,1,256]{2,1,0:T(1,128)}), f32[128,1,256]{2,1,0:T(1,128)S(1)}, u32[]{:S(2)}, u32[]{:S(2)}) async-start(f32[128,1,256]{2,1,0:T(1,128)} %reshape.1185), calls=%async_computation.1 | async-start | bytes 262144 | tf_op jit(solution)/shard_map/all_to_all | solution.py:66
  465.0 9.5 %all-to-all-done.1 = f32[128,1,256]{2,1,0:T(1,128)S(1)} async-done(((f32[128,1,256]{2,1,0:T(1,128)}), f32[128,1,256]{2,1,0:T(1,128)S(1)}, u32[]{:S(2)}, u32[]{:S(2)}) %all-to-all-start.1) | async-done | bytes 131104 | tf_op jit(solution)/shard_map/all_to_all | solution.py:66
  (537 shorter events, 202.0 us)
Async XLA Ops:
  0.6 23.4 %copy-start.22 = (f32[1,16,2048]{2,1,0:T(8,128)S(1)}, f32[1,16,2048]{2,1,0:T(8,128)}, u32[]{:S(2)}) copy-start(f32[1,16,2048]{2,1,0:T(8,128)} %param.117) | copy-start | bytes 393220
  1.7 23.2 %copy-start.20 = (f32[4,128,128]{2,1,0:T(8,128)S(1)}, f32[4,128,128]{2,1,0:T(8,128)}, u32[]{:S(2)}) copy-start(f32[4,128,128]{2,1,0:T(8,128)} %param.113) | copy-start | bytes 786436
  3.0 67.8 %collective-permute-start = (bf16[4,1,1,2048]{3,2,1,0:T(2,128)(2,1)S(1)}, bf16[4,1,1,2048]{3,2,1,0:T(2,128)(2,1)S(1)}, u32[]{:S(2)}, u32[]{:S(2)}) collective-permute-start(bf16[4,1,1,2048]{3,2,1,0:T(2,128)(2,1)S(1)} %get-tuple-element.1388), channel_id=1, source_target_pairs={{0,1},{1,2},{2,3},{3,4},{4,5},{5,6},{6,7},{7,8},{8,9},{9,10},{10,1... | collective-permute-start | bytes 49160 | tf_op jit(solution)/shard_map/ppermute | solution.py:22
  6.9 63.9 %collective-permute-start.1 = (bf16[4,1,1,2048]{3,2,1,0:T(2,128)(2,1)S(1)}, bf16[4,1,1,2048]{3,2,1,0:T(2,128)(2,1)S(1)}, u32[]{:S(2)}, u32[]{:S(2)}) collective-permute-start(bf16[4,1,1,2048]{3,2,1,0:T(2,128)(2,1)S(1)} %get-tuple-element.1389), channel_id=1, source_target_pairs={{1,0},{2,1},{3,2},{4,3},{5,4},{6,5},{7,6},{8,7},{9,8},{10,9},{11,1... | collective-permute-start | bytes 49160 | tf_op jit(solution)/shard_map/ppermute | solution.py:23
  15.6 64.7 %copy-start.60 = (s32[256]{0:T(256)}, s32[256]{0:T(256)S(1)}, u32[]{:S(2)}) copy-start(s32[256]{0:T(256)S(1)} %get-tuple-element.1420) | copy-start | bytes 3076
  31.3 32.9 %copy-start.62 = (s32[5]{0:T(128)S(1)}, s32[5]{0:T(128)}, u32[]{:S(2)}) copy-start(s32[5]{0:T(128)} %constant.563.clone.1) | copy-start | bytes 64
  31.3 39.4 %copy-start.5 = (bf16[64,64]{1,0:T(8,128)(2,1)S(1)}, bf16[64,64]{1,0:T(8,128)(2,1)}, u32[]{:S(2)}) copy-start(bf16[64,64]{1,0:T(8,128)(2,1)} %param.115) | copy-start | bytes 24580
  41.7 31.1 %all-to-all-start.2 = ((f32[128,1,256]{2,1,0:T(1,128)}), f32[128,1,256]{2,1,0:T(1,128)S(1)}, u32[]{:S(2)}, u32[]{:S(2)}) async-start(f32[128,1,256]{2,1,0:T(1,128)} %reshape.1187), calls=%async_computation.2 | async-start | bytes 262144 | tf_op jit(solution)/shard_map/all_to_all | solution.py:66
  61.5 16.8 %copy-start.32 = (s32[1024]{0:T(1024)}, s32[1024]{0:T(1024)S(1)}, u32[]{:S(2)}) copy-start(s32[1024]{0:T(1024)S(1)} %pad_clamp_fusion) | copy-start | bytes 12292
  82.0 24.2 %copy-start.12 = (bf16[3,3,4,64]{3,2,1,0:T(4,128)(2,1)S(1)}, bf16[3,3,4,64]{3,2,1,0:T(4,128)(2,1)}, u32[]{:S(2)}) copy-start(bf16[3,3,4,64]{3,2,1,0:T(4,128)(2,1)} %param.114) | copy-start | bytes 13828
  82.0 24.2 %copy-start.26 = (bf16[64]{0:T(256)(128)(2,1)S(1)}, bf16[64]{0:T(256)(128)(2,1)}, u32[]{:S(2)}) copy-start(bf16[64]{0:T(256)(128)(2,1)} %param.116) | copy-start | bytes 388
  82.6 23.6 %copy-start.23 = (f32[4,1,16,512]{3,2,1,0:T(8,128)S(1)}, f32[4,1,16,512]{3,2,1,0:T(8,128)}, u32[]{:S(2)}) copy-start(f32[4,1,16,512]{3,2,1,0:T(8,128)} %custom-call.12) | copy-start | bytes 393220
  93.0 24.6 %all-to-all-start.3 = ((f32[128,1,256]{2,1,0:T(1,128)}), f32[128,1,256]{2,1,0:T(1,128)S(1)}, u32[]{:S(2)}, u32[]{:S(2)}) async-start(f32[128,1,256]{2,1,0:T(1,128)} %reshape.1189), calls=%async_computation.3 | async-start | bytes 262144 | tf_op jit(solution)/shard_map/all_to_all | solution.py:66
  146.7 16.5 %copy-start.4 = (bf16[4,4,1,18,514]{4,1,3,2,0:T(4,128)(2,1)S(1)}, bf16[4,4,1,18,514]{4,1,3,2,0:T(4,128)(2,1)}, u32[]{:S(2)}) copy-start(bf16[4,4,1,18,514]{4,1,3,2,0:T(4,128)(2,1)} %copy-done.3) | copy-start | bytes 888196 | tf_op jit(solution)/shard_map/while
  146.7 16.5 %copy-start.14 = (bf16[3,3,4,64]{3,2,1,0:T(4,128)(2,1)S(1)}, bf16[3,3,4,64]{3,2,1,0:T(4,128)(2,1)}, u32[]{:S(2)}) copy-start(bf16[3,3,4,64]{3,2,1,0:T(4,128)(2,1)} %copy-done.13) | copy-start | bytes 13828 | tf_op jit(solution)/shard_map/while
  146.7 16.5 %copy-start.28 = (bf16[64]{0:T(256)(128)(2,1)S(1)}, bf16[64]{0:T(256)(128)(2,1)}, u32[]{:S(2)}) copy-start(bf16[64]{0:T(256)(128)(2,1)} %copy-done.27) | copy-start | bytes 388 | tf_op jit(solution)/shard_map/while
  185.7 16.6 %copy-start.4 = (bf16[4,4,1,18,514]{4,1,3,2,0:T(4,128)(2,1)S(1)}, bf16[4,4,1,18,514]{4,1,3,2,0:T(4,128)(2,1)}, u32[]{:S(2)}) copy-start(bf16[4,4,1,18,514]{4,1,3,2,0:T(4,128)(2,1)} %copy-done.3) | copy-start | bytes 888196 | tf_op jit(solution)/shard_map/while
  185.7 16.5 %copy-start.14 = (bf16[3,3,4,64]{3,2,1,0:T(4,128)(2,1)S(1)}, bf16[3,3,4,64]{3,2,1,0:T(4,128)(2,1)}, u32[]{:S(2)}) copy-start(bf16[3,3,4,64]{3,2,1,0:T(4,128)(2,1)} %copy-done.13) | copy-start | bytes 13828 | tf_op jit(solution)/shard_map/while
  185.7 16.5 %copy-start.28 = (bf16[64]{0:T(256)(128)(2,1)S(1)}, bf16[64]{0:T(256)(128)(2,1)}, u32[]{:S(2)}) copy-start(bf16[64]{0:T(256)(128)(2,1)} %copy-done.27) | copy-start | bytes 388 | tf_op jit(solution)/shard_map/while
  185.7 16.5 %copy-start.30 = (s32[4]{0:T(128)S(1)}, s32[4]{0:T(128)}, u32[]{:S(2)}) copy-start(s32[4]{0:T(128)} %get-tuple-element.1712) | copy-start | bytes 52 | tf_op jit(solution)/shard_map/while
  224.7 16.5 %copy-start.4 = (bf16[4,4,1,18,514]{4,1,3,2,0:T(4,128)(2,1)S(1)}, bf16[4,4,1,18,514]{4,1,3,2,0:T(4,128)(2,1)}, u32[]{:S(2)}) copy-start(bf16[4,4,1,18,514]{4,1,3,2,0:T(4,128)(2,1)} %copy-done.3) | copy-start | bytes 888196 | tf_op jit(solution)/shard_map/while
  263.7 16.5 %copy-start.4 = (bf16[4,4,1,18,514]{4,1,3,2,0:T(4,128)(2,1)S(1)}, bf16[4,4,1,18,514]{4,1,3,2,0:T(4,128)(2,1)}, u32[]{:S(2)}) copy-start(bf16[4,4,1,18,514]{4,1,3,2,0:T(4,128)(2,1)} %copy-done.3) | copy-start | bytes 888196 | tf_op jit(solution)/shard_map/while
  263.7 16.5 %copy-start.14 = (bf16[3,3,4,64]{3,2,1,0:T(4,128)(2,1)S(1)}, bf16[3,3,4,64]{3,2,1,0:T(4,128)(2,1)}, u32[]{:S(2)}) copy-start(bf16[3,3,4,64]{3,2,1,0:T(4,128)(2,1)} %copy-done.13) | copy-start | bytes 13828 | tf_op jit(solution)/shard_map/while
  263.7 16.5 %copy-start.28 = (bf16[64]{0:T(256)(128)(2,1)S(1)}, bf16[64]{0:T(256)(128)(2,1)}, u32[]{:S(2)}) copy-start(bf16[64]{0:T(256)(128)(2,1)} %copy-done.27) | copy-start | bytes 388 | tf_op jit(solution)/shard_map/while
  263.7 16.5 %copy-start.30 = (s32[4]{0:T(128)S(1)}, s32[4]{0:T(128)}, u32[]{:S(2)}) copy-start(s32[4]{0:T(128)} %get-tuple-element.1712) | copy-start | bytes 52 | tf_op jit(solution)/shard_map/while
  291.2 13.4 %collective-permute-start.2 = (bf16[64,1,1,2048]{3,0,2,1:T(8,128)(2,1)S(1)}, bf16[64,1,1,2048]{3,0,2,1:T(8,128)(2,1)S(1)}, u32[]{:S(2)}, u32[]{:S(2)}) collective-permute-start(bf16[64,1,1,2048]{3,0,2,1:T(8,128)(2,1)S(1)} %get-tuple-element.1375), channel_id=1, source_target_pairs={{0,1},{1,2},{2,3},{3,4},{4,5},{5,6},{6,7},{7,8},{8,9},{9,10},{10,1... | collective-permute-start | bytes 786440 | tf_op jit(solution)/shard_map/ppermute | solution.py:22
  293.4 11.2 %collective-permute-start.3 = (bf16[64,1,1,2048]{3,0,2,1:T(8,128)(2,1)S(1)}, bf16[64,1,1,2048]{3,0,2,1:T(8,128)(2,1)S(1)}, u32[]{:S(2)}, u32[]{:S(2)}) collective-permute-start(bf16[64,1,1,2048]{3,0,2,1:T(8,128)(2,1)S(1)} %get-tuple-element.1376), channel_id=1, source_target_pairs={{1,0},{2,1},{3,2},{4,3},{5,4},{6,5},{7,6},{8,7},{9,8},{10,9},{11,1... | collective-permute-start | bytes 786440 | tf_op jit(solution)/shard_map/ppermute | solution.py:23
  306.7 26.2 %copy-start.61 = (f32[4,64]{1,0:T(4,128)S(1)}, f32[4,64]{1,0:T(4,128)}, u32[]{:S(2)}) copy-start(f32[4,64]{1,0:T(4,128)} %get-tuple-element.1699) | copy-start | bytes 3076
  306.8 26.2 %copy-start.25 = (f32[4,3,3,4,64]{4,3,2,1,0:T(4,128)S(1)}, f32[4,3,3,4,64]{4,3,2,1,0:T(4,128)}, u32[]{:S(2)}) copy-start(f32[4,3,3,4,64]{4,3,2,1,0:T(4,128)} %get-tuple-element.1697) | copy-start | bytes 110596
  307.4 25.6 %copy-start.21 = (f32[4,64,64]{2,1,0:T(8,128)S(1)}, f32[4,64,64]{2,1,0:T(8,128)}, u32[]{:S(2)}) copy-start(f32[4,64,64]{2,1,0:T(8,128)} %get-tuple-element.1698) | copy-start | bytes 196612
  317.8 116.4 %all-to-all-start = ((f32[128,1,256]{2,1,0:T(1,128)}), f32[128,1,256]{2,1,0:T(1,128)S(1)}, u32[]{:S(2)}, u32[]{:S(2)}) async-start(f32[128,1,256]{2,1,0:T(1,128)} %reshape.1183), calls=%async_computation | async-start | bytes 262144 | tf_op jit(solution)/shard_map/all_to_all | solution.py:66
  454.5 20.1 %all-to-all-start.1 = ((f32[128,1,256]{2,1,0:T(1,128)}), f32[128,1,256]{2,1,0:T(1,128)S(1)}, u32[]{:S(2)}, u32[]{:S(2)}) async-start(f32[128,1,256]{2,1,0:T(1,128)} %reshape.1185), calls=%async_computation.1 | async-start | bytes 262144 | tf_op jit(solution)/shard_map/all_to_all | solution.py:66
  (66 other events, 388.2 us)
where the time goes:
time: 496 us; the launch traced here: 487 us
  local copies, waits for them, and re-layouts  164 us (33%)
  blocking collectives  101 us (20%)
  other arithmetic  87.3 us (18%)
  starting transfers between devices  65.5 us (13%)
  matrix products  42.9 us (9%)
  between operations  12.5 us (3%)
  waiting for transfers between devices  12 us (2%)
    psum x1, blocking collectives, on_device(): lax.psum((conv_total, mixing_total, flux_total), ('rep', 'sp'))  101 us
    scatter-add x28, local copies, waits for them, and re-layouts, closure_backward(): piece_cot.at[:, :, row_tap:row_tap + rows, col_tap:col_tap + cols].add(term)  76.6 us
    all_to_all x4, starting transfers between devices, relayout(): moved = lax.all_to_all(field, 'sp', split_axis=2, concat_axis=1, tiled=True)  56.8 us
    unnamed x4, other arithmetic  37.3 us
    unnamed x119, local copies, waits for them, and re-layouts  13.9 us
    another operation x15, other arithmetic  12.7 us
    dot_general x4, matrix products, closure_backward(): jnp.einsum('orxy,prxy->op', first_act, pre_second_cot, preferred_element_...  12.4 us
    all_to_all x4, waiting for transfers between devices, relayout(): moved = lax.all_to_all(field, 'sp', split_axis=2, concat_axis=1, tiled=True)  12 us
  transfers between devices with their start and end apart: 8, of which 3 were waited for; matrix products, arithmetic and copies ran while one was open for 11% of the time, Pallas kernels for 0%

commit v1 on v0

v1 whole, which is shorter than its diff:
```python
import math

import jax
import jax.numpy as jnp
from jax import lax
from jax.experimental import pallas as pl
from jax.experimental.pallas import tpu as pltpu
from jax.sharding import PartitionSpec as P

BF = jnp.bfloat16
F32 = jnp.float32
MESH = pl.DeviceIdType.MESH
SPAN = 128
ROWS = 16
HALF = 8
HID = 64
CIN = 4
PIECES = 12
WIDTH = 256
NCLS = 4
GROUP = SPAN // ROWS
DX, DZ, DYLO, DYHI, DCORE = 4, 8, 4, 2, 2
TIME_STEP = 0.5


def nt(a, b):
    return lax.dot_general(a, b, (((1,), (1,)), ((), ())), preferred_element_type=F32)


def nn(a, b):
    return lax.dot_general(a, b, (((1,), (0,)), ((), ())), preferred_element_type=F32)


def split2(v):
    hi = v.astype(BF)
    return hi, (v - hi.astype(F32)).astype(BF)


def split3(v):
    hi = v.astype(BF)
    rest = v - hi.astype(F32)
    mid = rest.astype(BF)
    return hi, mid, (rest - mid.astype(F32)).astype(BF)


def iota(shape, dim):
    return lax.broadcasted_iota(jnp.int32, shape, dim)


def onehot(cond):
    return jnp.where(cond, 1.0, 0.0).astype(BF)


def span_select(products, cls_ref, store):
    for k in range(products.shape[0] // ROWS):
        column = cls_ref[0, :, k : k + 1]
        result = products[k * ROWS : (k + 1) * ROWS, 0:SPAN]
        for group in range(1, NCLS):
            part = products[k * ROWS : (k + 1) * ROWS, group * SPAN : (group + 1) * SPAN]
            result = jnp.where(column == group, part, result)
        store(k, result)


def kernel(
    film_ref,
    evap_ref,
    mask_ref,
    fcls_ref,
    scls_ref,
    inv_ref,
    convw_ref,
    mixw_ref,
    fluxw_ref,
    cot_ref,
    final_ref,
    grad_ref,
    convg_ref,
    mixg_ref,
    fluxg_ref,
    invhi_ref,
    invlo_ref,
    invt_ref,
    gath_b,
    gath_f,
    halo_s,
    halo_r,
    padf_ref,
    x_ref,
    wb_ref,
    wct_ref,
    bdf_ref,
    bdb_ref,
    fwb_ref,
    fwc_ref,
    clsrow_ref,
    a1_ref,
    d1_ref,
    sa_ref,
    d2_ref,
    src_ref,
    back_ref,
    sg_ref,
    cacc_ref,
    macc_ref,
    facc_ref,
    tt_ref,
    tot_ref,
    rim_s,
    rim_r,
    w36_ref,
    g_ref,
    p1_ref,
    q1_ref,
    p2_ref,
    q2_ref,
    p3_ref,
    q3_ref,
    p4_ref,
    ag_ssem,
    ag_rsem,
    nb_ssem,
    nb_rsem,
    ar_ssem,
    ar_rsem,
):
    side = film_ref.shape[2]
    nblocks = side // WIDTH
    sp = lax.axis_index("sp")
    rep = lax.axis_index("rep")
    nsp = DYLO * DZ * DX
    x_at = sp % DX
    z_at = (sp // DX) % DZ
    ylo_at = sp // (DX * DZ)
    yhi_at = rep // DCORE
    core_at = rep % DCORE
    y_at = yhi_at * DYLO + ylo_at
    member = sp % GROUP
    first = sp - member

    def at(r, s):
        return {"rep": r, "sp": s}

    up = (sp + nsp - 1) % nsp
    down = (sp + 1) % nsp

    def group_peer(s):
        return at(rep, first + (member + s) % GROUP)

    j_at = core_at * DX + x_at

    def corner_peer(s):
        other = (j_at + s) % (DCORE * DX)
        return at(yhi_at * DCORE + other // DX, sp - x_at + other % DX)

    def z_peer(s):
        other = (z_at + s) % DZ
        return at(rep, (ylo_at * DZ + other) * DX + x_at)

    def y_peer(s):
        other = (y_at + s) % (DYHI * DYLO)
        return at(
            (other // DYLO) * DCORE + core_at,
            ((other % DYLO) * DZ + z_at) * DX + x_at,
        )

    barrier = pltpu.get_barrier_semaphore()
    peers = [at(rep, up), at(rep, down)]
    for s in range(1, 8):
        peers += [group_peer(s), corner_peer(s), z_peer(s), y_peer(s)]
    for peer in peers:
        pl.semaphore_signal(barrier, inc=1, device_id=peer, device_id_type=MESH)

    def remote(src, dst, ssem, rsem, peer):
        return pltpu.make_async_remote_copy(
            src_ref=src,
            dst_ref=dst,
            send_sem=ssem,
            recv_sem=rsem,
            device_id=peer,
            device_id_type=MESH,
        )

    inv = inv_ref[...].reshape(NCLS * SPAN, SPAN)
    inv_hi, inv_lo = split2(inv)
    invhi_ref[...] = inv_hi
    invlo_ref[...] = inv_lo
    for c in range(NCLS):
        t_hi, t_lo = split2(inv_ref[c].T)
        invt_ref[0, c] = t_hi
        invt_ref[1, c] = t_lo

    nspan = side // SPAN
    lines = jnp.concatenate(
        [cot_ref[0, :, k * SPAN : (k + 1) * SPAN] for k in range(nspan)], axis=0
    )
    l_hi, l_lo = split2(lines)
    right_hi = jnp.concatenate([inv_hi[c * SPAN : (c + 1) * SPAN] for c in range(NCLS)], axis=1)
    right_lo = jnp.concatenate([inv_lo[c * SPAN : (c + 1) * SPAN] for c in range(NCLS)], axis=1)
    products = nn(l_hi, right_hi) + nn(l_lo, right_hi) + nn(l_hi, right_lo)

    def store_back(k, value):
        back_ref[:, k * SPAN : (k + 1) * SPAN] = value.astype(BF)

    span_select(products, scls_ref, store_back)
    own_rows = pl.ds(pl.multiple_of(member * ROWS, ROWS), ROWS)
    gath_b[own_rows, :] = back_ref[...]

    film = film_ref[0]
    evap = evap_ref[0]
    maskf = mask_ref[0].astype(F32)
    for c, feature in enumerate((film, film * film, maskf, evap)):
        feature = feature.astype(BF).astype(F32)
        padf_ref[c, 1 : ROWS + 1, :] = feature
        padf_ref[c, ROWS + 2 :, :] = jnp.zeros((6, side), F32)
        halo_s[0, c : c + 1, :] = feature[0:1]
        halo_s[1, c : c + 1, :] = feature[ROWS - 1 :]

    pl.semaphore_wait(barrier, len(peers))

    halo_up = remote(halo_s.at[0], halo_r.at[1], nb_ssem.at[0], nb_rsem.at[0], at(rep, up))
    halo_down = remote(halo_s.at[1], halo_r.at[0], nb_ssem.at[1], nb_rsem.at[1], at(rep, down))
    halo_up.start()
    halo_down.start()

    def gather_copies(which, slab, gath):
        return [
            remote(
                slab,
                gath.at[own_rows],
                ag_ssem.at[which, s - 1],
                ag_rsem.at[which, s - 1],
                group_peer(s),
            )
            for s in range(1, GROUP)
        ]

    back_copies = gather_copies(0, back_ref, gath_b)
    for copy in back_copies:
        copy.start()

    w36_ref[...] = jnp.zeros_like(w36_ref)
    for a in range(3):
        for b in range(3):
            k = (a * 3 + b) * CIN
            w36_ref[k : k + CIN, 0:HID] = convw_ref[a, b].astype(F32)
    w_t = w36_ref[...].T[:HID].astype(BF)
    k_at = iota((SPAN, WIDTH), 0)
    col = iota((SPAN, WIDTH), 1)
    piece = col // 16
    tap_row = col % 16
    wanted = (tap_row * 3 + piece % 3) * CIN + piece // 3
    pick = (k_at == wanted) & (tap_row < 3) & (piece < PIECES)
    band0 = nn(w_t, onehot(pick))
    band = jnp.concatenate(
        [band0] + [pltpu.roll(band0, r, axis=1) for r in range(1, HALF)], axis=0
    )
    wb_ref[...] = band.astype(BF)
    wct_ref[...] = band[:, :SPAN].T[:96].astype(BF)
    mix = mixw_ref[...]
    tile4 = onehot(iota((HID, WIDTH), 1) % HID == iota((HID, WIDTH), 0))
    wide = nn(mix, tile4)
    tall = jnp.concatenate([wide] * 4, axis=0)
    same = iota((WIDTH, WIDTH), 0) // HID == iota((WIDTH, WIDTH), 1) // HID
    diag = jnp.where(same, tall, 0.0)
    bdb_ref[...] = diag.astype(BF)
    bdf_ref[...] = diag.T.astype(BF)
    fw = fluxw_ref[...]
    tile8 = onehot(iota((HID, HALF * HID), 1) % HID == iota((HID, HALF * HID), 0))
    fw_wide = nn(jnp.broadcast_to(fw, (16, HID)), tile8)
    own = iota((16, HALF * HID), 1) // HID == iota((16, HALF * HID), 0)
    fwb_ref[...] = jnp.where(own, fw_wide, 0.0).astype(BF)
    eye = iota((HID, HID), 0) == iota((HID, HID), 1)
    fw_col = jnp.sum(
        jnp.where(eye, jnp.broadcast_to(fw.astype(F32), (HID, HID)), 0.0), axis=1, keepdims=True
    )
    fwc_ref[...] = jnp.broadcast_to(fw_col, (HID, WIDTH))

    fcls = fcls_ref[0].astype(F32).astype(BF)
    pick_span = onehot(iota((16, nspan), 1) == sp // GROUP)
    clsrow_ref[...] = nt(pick_span, fcls)

    halo_up.wait()
    halo_down.wait()
    for c in range(CIN):
        padf_ref[c, 0:1, :] = jnp.where(sp > 0, halo_r[0, c : c + 1, :], 0.0)
        padf_ref[c, ROWS + 1 : ROWS + 2, :] = jnp.where(
            sp < nsp - 1, halo_r[1, c : c + 1, :], 0.0
        )
    lane = iota((24, side), 1)
    for c in range(CIN):
        middle = padf_ref[c]
        left = jnp.where(lane == 0, 0.0, pltpu.roll(middle, 1, axis=1))
        right = jnp.where(lane == side - 1, 0.0, pltpu.roll(middle, side - 1, axis=1))
        for b, values in enumerate((left, middle, right)):
            s = (c * 3 + b) * 16
            for h in range(2):
                x_ref[h, s : s + 16, :] = values[HALF * h : HALF * h + 16].astype(BF)

    def forward(i, carry):
        cols = pl.ds(pl.multiple_of(i * WIDTH, WIDTH), WIDTH)
        sources = []
        for h in range(2):
            t1 = jnp.tanh(nn(wb_ref[:, : PIECES * 16], x_ref[h, :, cols]))
            a1 = t1.astype(BF)
            a1_ref[h, :, cols] = a1
            d1_ref[h, :, cols] = 1.0 - t1 * t1
            t2 = jnp.tanh(
                jnp.concatenate([nn(bdf_ref[...], a1[:WIDTH]), nn(bdf_ref[...], a1[WIDTH:])], axis=0)
            )
            sa = t2.astype(BF)
            sa_ref[h, :, cols] = sa
            d2_ref[h, :, cols] = 1.0 - t2 * t2
            flux = nn(fwb_ref[...], sa)[:HALF]
            rows = slice(HALF * h, HALF * h + HALF)
            drain = mask_ref[0, rows, cols].astype(F32) * evap_ref[0, rows, cols]
            sources.append(film_ref[0, rows, cols] + TIME_STEP * (flux - drain))
        src_ref[:, cols] = jnp.concatenate(sources, axis=0).astype(BF)
        return carry

    lax.fori_loop(0, nblocks, forward, 0)
    gath_f[own_rows, :] = src_ref[...]
    source_copies = gather_copies(1, src_ref, gath_f)
    for copy in source_copies:
        copy.start()

    def along_first(left, gathered, cols):
        both = nn(left, gathered[:, cols])
        total = both[: NCLS * ROWS] + both[NCLS * ROWS :]
        classes = clsrow_ref[:, cols]
        result = total[:ROWS]
        for c in range(1, NCLS):
            result = jnp.where(classes == c, total[c * ROWS : (c + 1) * ROWS], result)
        return result

    for s in range(1, GROUP):
        remote(
            back_ref,
            gath_b.at[pl.ds(pl.multiple_of(((member + GROUP - s) % GROUP) * ROWS, ROWS), ROWS)],
            ag_ssem.at[0, s - 1],
            ag_rsem.at[0, s - 1],
            group_peer(s),
        ).wait()
    left_t = jnp.concatenate(
        [invt_ref[n, c, own_rows, :] for n in range(2) for c in range(NCLS)], axis=0
    )
    wide_cols = min(512, side)

    def adjoint(i, carry):
        cols = pl.ds(pl.multiple_of(i * wide_cols, wide_cols), wide_cols)
        sg_ref[:, cols] = along_first(left_t, gath_b, cols)
        return carry

    lax.fori_loop(0, side // wide_cols, adjoint, 0)

    cacc_ref[...] = jnp.zeros_like(cacc_ref)
    macc_ref[...] = jnp.zeros_like(macc_ref)
    facc_ref[...] = jnp.zeros_like(facc_ref)

    def backward(i, carry):
        cols = pl.ds(pl.multiple_of(i * WIDTH, WIDTH), WIDTH)
        flux_sum = facc_ref[...]
        mixing = macc_ref[...]
        for h in range(2):
            flux_cot = TIME_STEP * sg_ref[HALF * h : HALF * h + HALF, cols]
            cots = []
            for r in range(HALF):
                of = slice(r * HID, (r + 1) * HID)
                row = jnp.broadcast_to(flux_cot[r : r + 1], (HID, WIDTH))
                flux_sum = flux_sum + sa_ref[h, of, cols].astype(F32) * row
                second_cot = (fwc_ref[...] * row).astype(BF).astype(F32)
                pre = (second_cot * d2_ref[h, of, cols]).astype(BF)
                mixing = mixing + nt(a1_ref[h, of, cols], pre)
                cots.append(pre)
            firsts = []
            for q in range(2):
                first_cot = nn(bdb_ref[...], jnp.concatenate(cots[4 * q : 4 * q + 4], axis=0))
                first_cot = first_cot.astype(BF).astype(F32)
                firsts.append((first_cot * d1_ref[h, WIDTH * q : WIDTH * q + WIDTH, cols]).astype(BF))
            pre_first = jnp.concatenate(firsts, axis=0)
            a1_ref[h, :, cols] = pre_first
            cacc_ref[...] += nt(pre_first, x_ref[h, :, cols])
        facc_ref[...] = flux_sum
        macc_ref[...] = mixing
        return carry

    lax.fori_loop(0, nblocks, backward, 0)

    whole = jnp.concatenate(
        [cacc_ref[...], jnp.zeros((HALF * HID, WIDTH - PIECES * 16), F32)], axis=1
    )
    taps = whole[:HID]
    for r in range(1, HALF):
        taps = taps + pltpu.roll(whole[r * HID : (r + 1) * HID], WIDTH - r, axis=1)
    k_at = iota((HID, WIDTH), 0)
    col = iota((HID, WIDTH), 1)
    piece = col // 16
    tap_row = col % 16
    wanted = (tap_row * 3 + piece % 3) * CIN + piece // 3
    pick = onehot((k_at == wanted) & (tap_row < 3) & (piece < PIECES))
    ones_row = onehot(k_at == 9 * CIN)
    low = jnp.zeros((HID, WIDTH), BF)
    right = jnp.zeros((HID, 2 * HID), F32)
    for t, f in zip(split3(taps), split3(facc_ref[...])):
        right = right + nt(pick, jnp.concatenate([low, t], axis=0))
        right = right + nt(ones_row, jnp.concatenate([low, f], axis=0))
    g_ref[...] = right
    g_ref[:, 0:HID] = macc_ref[...]

    own_block = pl.ds(pl.multiple_of(j_at * 8, 8), 8)
    p1_ref[j_at] = g_ref[own_block, :]
    stage1 = []
    for s in range(1, 8):
        other = (j_at + s) % 8
        stage1.append(
            remote(
                g_ref.at[pl.ds(pl.multiple_of(other * 8, 8), 8)],
                p1_ref.at[j_at],
                ar_ssem.at[0, s - 1],
                ar_rsem.at[0, s - 1],
                corner_peer(s),
            )
        )
    for copy in stage1:
        copy.start()

    def features_back(i, carry):
        cols = pl.ds(pl.multiple_of(i * WIDTH, WIDTH), WIDTH)
        for h in range(2):
            tt_ref[h, :, cols] = nn(wct_ref[...], a1_ref[h, :, cols])
        return carry

    lax.fori_loop(0, nblocks, features_back, 0)

    def finish(stage, slots, at_index, source, send_peer):
        for s in range(1, 8):
            remote(
                source,
                slots.at[(at_index + 8 - s) % 8],
                ar_ssem.at[stage, s - 1],
                ar_rsem.at[stage, s - 1],
                send_peer(s),
            ).wait()

    def begin(stage, slots, at_index, source, send_peer):
        for s in range(1, 8):
            remote(
                source,
                slots.at[at_index],
                ar_ssem.at[stage, s - 1],
                ar_rsem.at[stage, s - 1],
                send_peer(s),
            ).start()

    def summed(slots):
        total = slots[0]
        for n in range(1, 8):
            total = total + slots[n]
        return total

    finish(0, p1_ref, j_at, g_ref.at[own_block], corner_peer)
    q1_ref[...] = summed(p1_ref)
    p2_ref[z_at] = q1_ref[...]
    begin(1, p2_ref, z_at, q1_ref, z_peer)

    lane = iota((16, side), 1)
    for c in range(2):
        parts = []
        for h in range(2):
            s = c * 48
            left = jnp.where(lane == side - 1, 0.0, pltpu.roll(tt_ref[h, s : s + 16, :], side - 1, axis=1))
            right = jnp.where(lane == 0, 0.0, pltpu.roll(tt_ref[h, s + 32 : s + 48, :], 1, axis=1))
            parts.append(left + tt_ref[h, s + 16 : s + 32, :] + right)
        tot_ref[c, 0:8, :] = parts[0][0:8]
        tot_ref[c, 8:16, :] = parts[0][8:16] + parts[1][0:8]
        tot_ref[c, 16:24, :] = parts[1][8:16]
        rim_s[0, c : c + 1, :] = parts[0][0:1]
        rim_s[1, c : c + 1, :] = parts[1][9:10]
    rim_up = remote(rim_s.at[0], rim_r.at[1], nb_ssem.at[2], nb_rsem.at[2], at(rep, up))
    rim_down = remote(rim_s.at[1], rim_r.at[0], nb_ssem.at[3], nb_rsem.at[3], at(rep, down))
    rim_up.start()
    rim_down.start()

    for s in range(1, GROUP):
        remote(
            src_ref,
            gath_f.at[pl.ds(pl.multiple_of(((member + GROUP - s) % GROUP) * ROWS, ROWS), ROWS)],
            ag_ssem.at[1, s - 1],
            ag_rsem.at[1, s - 1],
            group_peer(s),
        ).wait()
    left_f = jnp.concatenate(
        [
            half[pl.ds(pl.multiple_of(c * SPAN + member * ROWS, ROWS), ROWS), :]
            for half in (invhi_ref, invlo_ref)
            for c in range(NCLS)
        ],
        axis=0,
    )
    pieces = []
    for i in range(side // wide_cols):
        across = along_first(left_f, gath_f, slice(i * wide_cols, (i + 1) * wide_cols))
        for k in range(wide_cols // SPAN):
            pieces.append(across[:, k * SPAN : (k + 1) * SPAN])
    l_hi, l_lo = split2(jnp.concatenate(pieces, axis=0))
    f_hi = invhi_ref[...]
    products = nt(l_hi, f_hi) + nt(l_lo, f_hi) + nt(l_hi, invlo_ref[...])

    def store_final(k, value):
        final_ref[0, :, k * SPAN : (k + 1) * SPAN] = value

    span_select(products, scls_ref, store_final)

    finish(1, p2_ref, z_at, q1_ref, z_peer)
    q2_ref[...] = summed(p2_ref)
    p3_ref[y_at] = q2_ref[...]
    begin(2, p3_ref, y_at, q2_ref, y_peer)

    rim_up.wait()
    rim_down.wait()
    for c in range(2):
        tot_ref[c, 1:2, :] += jnp.where(sp > 0, rim_r[0, c : c + 1, :], 0.0)
        tot_ref[c, ROWS : ROWS + 1, :] += jnp.where(sp < nsp - 1, rim_r[1, c : c + 1, :], 0.0)
    cot0 = tot_ref[0, 1 : ROWS + 1, :].astype(BF).astype(F32)
    cot1 = tot_ref[1, 1 : ROWS + 1, :].astype(BF).astype(F32)
    grad_ref[0] = sg_ref[...] + cot0 + 2.0 * film_ref[0] * cot1

    finish(2, p3_ref, y_at, q2_ref, y_peer)
    q3_ref[...] = summed(p3_ref)
    p4_ref[j_at] = q3_ref[...]
    begin(3, p4_ref, j_at, q3_ref, corner_peer)
    finish(3, p4_ref, j_at, q3_ref, corner_peer)
    scale = 1.0 / math.sqrt(DYHI * DCORE * side * side)
    result = p4_ref[...].reshape(HID, 2 * HID) * scale
    mixg_ref[...] = result[:, :HID]
    other = pltpu.roll(result, HID, axis=1)[:, :HID]
    for a in range(3):
        for b in range(3):
            k = (a * 3 + b) * CIN
            convg_ref[a, b] = other[k : k + CIN]
    fluxg_ref[...] = other[9 * CIN : 9 * CIN + 1]


def on_device(film, evap, mask, fcls, scls, inv, convw, mixw, fluxw, cot):
    side = film.shape[2]
    rows = film.shape[1]
    vmem = pl.BlockSpec(memory_space=pltpu.VMEM)
    outs = pl.pallas_call(
        kernel,
        out_shape=(
            jax.ShapeDtypeStruct(film.shape, F32),
            jax.ShapeDtypeStruct(film.shape, F32),
            jax.ShapeDtypeStruct(convw.shape, F32),
            jax.ShapeDtypeStruct(mixw.shape, F32),
            jax.ShapeDtypeStruct((1, HID), F32),
        ),
        in_specs=[vmem] * 10,
        out_specs=(vmem,) * 5,
        scratch_shapes=[
            pltpu.VMEM((NCLS * SPAN, SPAN), BF),
            pltpu.VMEM((NCLS * SPAN, SPAN), BF),
            pltpu.VMEM((2, NCLS, SPAN, SPAN), BF),
            pltpu.VMEM((SPAN, side), BF),
            pltpu.VMEM((SPAN, side), BF),
            pltpu.VMEM((2, CIN, side), F32),
            pltpu.VMEM((2, CIN, side), F32),
            pltpu.VMEM((CIN, 24, side), F32),
            pltpu.VMEM((2, PIECES * 16, side), BF),
            pltpu.VMEM((HALF * HID, WIDTH), BF),
            pltpu.VMEM((96, HALF * HID), BF),
            pltpu.VMEM((WIDTH, WIDTH), BF),
            pltpu.VMEM((WIDTH, WIDTH), BF),
            pltpu.VMEM((16, HALF * HID), BF),
            pltpu.VMEM((HID, WIDTH), F32),
            pltpu.VMEM((16, side), F32),
            pltpu.VMEM((2, HALF * HID, side), BF),
            pltpu.VMEM((2, HALF * HID, side), F32),
            pltpu.VMEM((2, HALF * HID, side), BF),
            pltpu.VMEM((2, HALF * HID, side), F32),
            pltpu.VMEM((rows, side), BF),
            pltpu.VMEM((rows, side), BF),
            pltpu.VMEM((rows, side), F32),
            pltpu.VMEM((HALF * HID, PIECES * 16), F32),
            pltpu.VMEM((HID, HID), F32),
            pltpu.VMEM((HID, WIDTH), F32),
            pltpu.VMEM((2, 96, side), F32),
            pltpu.VMEM((2, 24, side), F32),
            pltpu.VMEM((2, 2, side), F32),
            pltpu.VMEM((2, 2, side), F32),
            pltpu.VMEM((SPAN, SPAN), F32),
            pltpu.VMEM((HID, 2 * HID), F32),
            pltpu.VMEM((8, 8, 2 * HID), F32),
            pltpu.VMEM((8, 2 * HID), F32),
            pltpu.VMEM((8, 8, 2 * HID), F32),
            pltpu.VMEM((8, 2 * HID), F32),
            pltpu.VMEM((8, 8, 2 * HID), F32),
            pltpu.VMEM((8, 2 * HID), F32),
            pltpu.VMEM((8, 8, 2 * HID), F32),
            pltpu.SemaphoreType.DMA((2, 7)),
            pltpu.SemaphoreType.DMA((2, 7)),
            pltpu.SemaphoreType.DMA((4,)),
            pltpu.SemaphoreType.DMA((4,)),
            pltpu.SemaphoreType.DMA((4, 7)),
            pltpu.SemaphoreType.DMA((4, 7)),
        ],
        compiler_params=pltpu.CompilerParams(
            collective_id=0, has_side_effects=True, vmem_limit_bytes=60 * 1024 * 1024
        ),
    )(film, evap, mask, fcls, scls, inv, convw, mixw, fluxw.reshape(1, HID), cot)
    return outs[0], outs[1], outs[2], outs[3], outs[4].reshape(HID)


def solution(mesh):
    sizes = dict(mesh.shape)
    assert sizes == {"rep": DYHI * DCORE, "sp": DYLO * DZ * DX}
    return jax.shard_map(
        on_device,
        mesh=mesh,
        in_specs=(
            P("rep", "sp", None),
            P("rep", "sp", None),
            P("rep", "sp", None),
            P("rep", None, None),
            P("rep", "sp", None),
            P(),
            P(),
            P(),
            P(),
            P("rep", "sp", None),
        ),
        out_specs=(P("rep", "sp", None), P("rep", "sp", None), P(), P(), P()),
        check_vma=False,
    )
```

time: 496 us -> 63.4 us (0.13); the launches traced: 487 us -> 63 us
  local copies, waits for them, and re-layouts: 164 us -> 6.48 us
  blocking collectives: 101 us -> 0 us
  other arithmetic: 87.3 us -> 0 us
  starting transfers between devices: 65.5 us -> 0 us
  Pallas kernels: 0 us -> 55.9 us
  matrix products: 42.9 us -> 0 us
  waiting for transfers between devices: 12 us -> 0 us
  between operations: 12.5 us -> 0.65 us
    psum x1 -> x0, blocking collectives: 101 us -> none  [on_device(): lax.psum((conv_total, mixing_total, flux_total), ('rep', 'sp'))]
    scatter-add x29 -> x0, local copies, waits for them, and re-layouts: 80.9 us -> none  [the longest x28 76.6 us: closure_backward(): piece_cot.at[:, :, row_tap:row_tap + rows, col_tap:col_tap + cols].add(term)]
    all_to_all x4 -> x0, starting transfers between devices: 56.8 us -> none  [relayout(): moved = lax.all_to_all(field, 'sp', split_axis=2, concat_axis=1, tiled=True)]
    pallas_call x0 -> x1, Pallas kernels: none -> 55.9 us  [on_device(): pl.pallas_call(kernel, out_shape=(jax.ShapeDtypeStruct(film.shape, F32),...]
    dot_general x60 -> x0, matrix products: 42.9 us -> none  [the longest x4 12.4 us: closure_backward(): jnp.einsum('orxy,prxy->op', first_act, pre_second_cot, preferred_element_...]
    unnamed x4 -> x0, other arithmetic: 37.3 us -> none
    another operation x17 -> x0, other arithmetic: 13.9 us -> none
    all_to_all x4 -> x0, waiting for transfers between devices: 12 us -> none  [relayout(): moved = lax.all_to_all(field, 'sp', split_axis=2, concat_axis=1, tiled=True)]
  transfers between devices with their start and end apart: 8 -> 0, of which waited for: 3 -> 0; matrix products, arithmetic and copies ran while one was open for 11% -> 0% of each run, Pallas kernels for 0% -> 0%
where the time goes in v1:
time: 63.4 us; the launch traced here: 63 us
  Pallas kernels  55.9 us (88%)
  local copies, waits for them, and re-layouts  6.48 us (10%)
  between operations  0.65 us (1%)
    pallas_call x1, Pallas kernels, on_device(): pl.pallas_call(kernel, out_shape=(jax.ShapeDtypeStruct(film.shape, F32),...  55.9 us
    unnamed x14, local copies, waits for them, and re-layouts  6.48 us

profile of v1, /device:TPU:1, one launch (start us, length us, event | category | flops | bytes accessed | tf_op | source)
XLA Modules:
  0.0 63.0 jit_solution(16618103240505469217)
XLA Ops:
  0.6 2.2 %copy.15.fcls_ref = s32[1,2048,16]{2,1,0:T(8,128)} copy(s32[1,2048,16]{1,2,0:T(8,128)} %param.13) | data formatting | bytes 262144 | tf_op args[3]
  2.8 55.9 %shard_map.137 = (f32[1,16,2048]{2,1,0:T(8,128)}, f32[1,16,2048]{2,1,0:T(8,128)}, f32[3,3,4,64]{3,2,1,0:T(4,128)}, f32[64,64]{1,0:T(8,128)}, f32[1,64]{1,0:T(1,128)}) custom-call(f32[1,16,2048]{2,1,0:T(8,128)} %film_ref.1, f32[1,16,2048]{2,1,0:T(8,128)} %evap_ref.1, s32[1,16,2048]{2,1,0:T(8,128)} %mask_ref.1, s32[1,2048,16]{2,1,0:T(8,128)} %copy.15.fcls_ref, ...), custom_call_target="tpu_custom_call" | custom-call | tf_op jit(solution)/shard_map/pallas_call | solution.py:547
  58.8 0.0 copy-start
  58.8 1.6 %copy.21 = f32[1,16,2048]{2,1,0:T(8,128)} copy(f32[1,16,2048]{2,1,0:T(8,128)} %get-tuple-element.20) | data formatting | bytes 262144
  60.4 0.0 copy-done
  60.4 0.0 copy-start.2
  60.4 0.7 %copy.22 = f32[1,16,2048]{2,1,0:T(8,128)} copy(f32[1,16,2048]{2,1,0:T(8,128)S(1)} %copy-done) | data formatting | bytes 262144
  61.0 0.1 copy-done.2
  61.1 0.0 copy-start.1
  61.1 0.6 copy.23
  61.7 0.2 copy-done.1
  61.9 0.0 copy-start.3
  61.9 0.6 copy.24
  62.5 0.1 copy-done.3
  62.5 0.5 copy.25
Async XLA Ops:
  58.8 1.6 %copy-start = (f32[1,16,2048]{2,1,0:T(8,128)S(1)}, f32[1,16,2048]{2,1,0:T(8,128)}, u32[]{:S(2)}) copy-start(f32[1,16,2048]{2,1,0:T(8,128)} %get-tuple-element.21) | copy-start | bytes 393220
  60.4 0.7 %copy-start.2 = (f32[3,3,4,64]{3,2,1,0:T(4,128)S(1)}, f32[3,3,4,64]{3,2,1,0:T(4,128)}, u32[]{:S(2)}) copy-start(f32[3,3,4,64]{3,2,1,0:T(4,128)} %get-tuple-element.22) | copy-start | bytes 27652
  61.1 0.8 %copy-start.1 = (f32[64,64]{1,0:T(8,128)S(1)}, f32[64,64]{1,0:T(8,128)}, u32[]{:S(2)}) copy-start(f32[64,64]{1,0:T(8,128)} %get-tuple-element.23) | copy-start | bytes 49156
  61.9 0.7 %copy-start.3 = (f32[1,64]{1,0:T(1,128)S(1)}, f32[1,64]{1,0:T(1,128)}, u32[]{:S(2)}) copy-start(f32[1,64]{1,0:T(1,128)} %get-tuple-element.14) | copy-start | bytes 772

commit v2 on v1

--- a/solution.py
+++ b/solution.py
@@ -62,6 +62,19 @@
 
 
 def kernel(
+    film_hbm,
+    evap_hbm,
+    mask_hbm,
+    fcls_hbm,
+    scls_hbm,
+    inv_hbm,
+    convw_hbm,
+    mixw_hbm,
+    fluxw_hbm,
+    cot_hbm,
+    final_hbm,
+    grad_hbm,
+    gsum_hbm,
     film_ref,
     evap_ref,
     mask_ref,
@@ -74,14 +87,10 @@
     cot_ref,
     final_ref,
     grad_ref,
-    convg_ref,
-    mixg_ref,
-    fluxg_ref,
-    invhi_ref,
-    invlo_ref,
-    invt_ref,
-    gath_b,
-    gath_f,
+    gsum_ref,
+    invs_ref,
+    recv_ref,
+    mid_ref,
     halo_s,
     halo_r,
     padf_ref,
@@ -92,14 +101,15 @@
     bdb_ref,
     fwb_ref,
     fwc_ref,
-    clsrow_ref,
     a1_ref,
     d1_ref,
     sa_ref,
-    d2_ref,
+    u_ref,
+    v_ref,
     src_ref,
     back_ref,
     sg_ref,
+    across_ref,
     cacc_ref,
     macc_ref,
     facc_ref,
@@ -116,6 +126,8 @@
     p3_ref,
     q3_ref,
     p4_ref,
+    in_sem,
+    out_sem,
     ag_ssem,
     ag_rsem,
     nb_ssem,
@@ -123,6 +135,25 @@
     ar_ssem,
     ar_rsem,
 ):
+    inputs = [
+        pltpu.make_async_copy(hbm, ref, in_sem.at[n])
+        for n, (hbm, ref) in enumerate(
+            (
+                (cot_hbm, cot_ref),
+                (inv_hbm, inv_ref),
+                (scls_hbm, scls_ref),
+                (film_hbm, film_ref),
+                (evap_hbm, evap_ref),
+                (mask_hbm, mask_ref),
+                (fcls_hbm, fcls_ref),
+                (convw_hbm, convw_ref),
+                (mixw_hbm, mixw_ref),
+                (fluxw_hbm, fluxw_ref),
+            )
+        )
+    ]
+    for copy in inputs:
+        copy.start()
     side = film_ref.shape[2]
     nblocks = side // WIDTH
     sp = lax.axis_index("sp")
@@ -180,14 +211,16 @@
             device_id_type=MESH,
         )
 
-    inv = inv_ref[...].reshape(NCLS * SPAN, SPAN)
-    inv_hi, inv_lo = split2(inv)
-    invhi_ref[...] = inv_hi
-    invlo_ref[...] = inv_lo
+    for copy in inputs[:3]:
+        copy.wait()
+    inv_hi, inv_lo = split2(inv_ref[...].reshape(NCLS * SPAN, SPAN))
     for c in range(NCLS):
+        of = slice(c * SPAN, (c + 1) * SPAN)
         t_hi, t_lo = split2(inv_ref[c].T)
-        invt_ref[0, c] = t_hi
-        invt_ref[1, c] = t_lo
+        invs_ref[0, 0, c] = t_hi
+        invs_ref[0, 1, c] = t_lo
+        invs_ref[1, 0, c] = inv_hi[of]
+        invs_ref[1, 1, c] = inv_lo[of]
 
     nspan = side // SPAN
     lines = jnp.concatenate(
@@ -203,7 +236,68 @@
 
     span_select(products, scls_ref, store_back)
     own_rows = pl.ds(pl.multiple_of(member * ROWS, ROWS), ROWS)
-    gath_b[own_rows, :] = back_ref[...]
+    chunk = side // GROUP
+
+    def columns_of(n):
+        return pl.ds(pl.multiple_of(n * chunk, chunk), chunk)
+
+    def rows_of(n):
+        return pl.ds(pl.multiple_of(n * ROWS, ROWS), ROWS)
+
+    def from_peer(s):
+        return (member + GROUP - s) % GROUP
+
+    def span_out(which, field):
+        recv_ref[which, own_rows, :] = field[:, columns_of(member)]
+        for s in range(1, GROUP):
+            remote(
+                field.at[:, columns_of((member + s) % GROUP)],
+                recv_ref.at[which, own_rows],
+                ag_ssem.at[2 * which, s - 1],
+                ag_rsem.at[2 * which, s - 1],
+                group_peer(s),
+            ).start()
+
+    def span_solve(which, field, result):
+        for s in range(1, GROUP):
+            remote(
+                field.at[:, columns_of((member + s) % GROUP)],
+                recv_ref.at[which, rows_of(from_peer(s))],
+                ag_ssem.at[2 * which, s - 1],
+                ag_rsem.at[2 * which, s - 1],
+                group_peer(s),
+            ).wait()
+        values = recv_ref[which]
+        line_cls = fcls_ref[0, :, columns_of(member)]
+        own_span = iota(line_cls.shape, 0) == sp // GROUP
+        classes = jnp.sum(jnp.where(own_span, line_cls, 0), axis=0, keepdims=True)
+        solved = None
+        for c in range(NCLS):
+            product = nn(invs_ref[which, 0, c], values) + nn(invs_ref[which, 1, c], values)
+            solved = product if c == 0 else jnp.where(classes == c, product, solved)
+        mid_ref[which] = solved.astype(BF)
+        result[:, columns_of(member)] = mid_ref[which, own_rows, :]
+        for s in range(1, GROUP):
+            remote(
+                mid_ref.at[which, rows_of((member + s) % GROUP)],
+                result.at[:, columns_of(member)],
+                ag_ssem.at[2 * which + 1, s - 1],
+                ag_rsem.at[2 * which + 1, s - 1],
+                group_peer(s),
+            ).start()
+
+    def span_in(which, result):
+        for s in range(1, GROUP):
+            remote(
+                mid_ref.at[which, rows_of((member + s) % GROUP)],
+                result.at[:, columns_of(from_peer(s))],
+                ag_ssem.at[2 * which + 1, s - 1],
+                ag_rsem.at[2 * which + 1, s - 1],
+                group_peer(s),
+            ).wait()
+
+    for copy in inputs[3:]:
+        copy.wait()
 
     film = film_ref[0]
     evap = evap_ref[0]
@@ -222,21 +316,7 @@
     halo_up.start()
     halo_down.start()
 
-    def gather_copies(which, slab, gath):
-        return [
-            remote(
-                slab,
-                gath.at[own_rows],
-                ag_ssem.at[which, s - 1],
-                ag_rsem.at[which, s - 1],
-                group_peer(s),
-            )
-            for s in range(1, GROUP)
-        ]
-
-    back_copies = gather_copies(0, back_ref, gath_b)
-    for copy in back_copies:
-        copy.start()
+    span_out(0, back_ref)
 
     w36_ref[...] = jnp.zeros_like(w36_ref)
     for a in range(3):
@@ -273,11 +353,7 @@
     fw_col = jnp.sum(
         jnp.where(eye, jnp.broadcast_to(fw.astype(F32), (HID, HID)), 0.0), axis=1, keepdims=True
     )
-    fwc_ref[...] = jnp.broadcast_to(fw_col, (HID, WIDTH))
-
-    fcls = fcls_ref[0].astype(F32).astype(BF)
-    pick_span = onehot(iota((16, nspan), 1) == sp // GROUP)
-    clsrow_ref[...] = nt(pick_span, fcls)
+    fwc_ref[...] = jnp.concatenate([jnp.broadcast_to(fw_col, (HID, WIDTH))] * 4, axis=0)
 
     halo_up.wait()
     halo_down.wait()
@@ -303,13 +379,17 @@
             t1 = jnp.tanh(nn(wb_ref[:, : PIECES * 16], x_ref[h, :, cols]))
             a1 = t1.astype(BF)
             a1_ref[h, :, cols] = a1
-            d1_ref[h, :, cols] = 1.0 - t1 * t1
-            t2 = jnp.tanh(
-                jnp.concatenate([nn(bdf_ref[...], a1[:WIDTH]), nn(bdf_ref[...], a1[WIDTH:])], axis=0)
-            )
-            sa = t2.astype(BF)
+            d1_ref[h] = 1.0 - t1 * t1
+            actives = []
+            for q in range(2):
+                of = slice(q * WIDTH, (q + 1) * WIDTH)
+                t2 = jnp.tanh(nn(bdf_ref[...], a1[of]))
+                actives.append(t2.astype(BF))
+                u = (fwc_ref[...] * (1.0 - t2 * t2)).astype(BF)
+                u_ref[h, of, cols] = u
+                v_ref[h, of, cols] = (d1_ref[h, of, :] * nn(bdb_ref[...], u)).astype(BF)
+            sa = jnp.concatenate(actives, axis=0)
             sa_ref[h, :, cols] = sa
-            d2_ref[h, :, cols] = 1.0 - t2 * t2
             flux = nn(fwb_ref[...], sa)[:HALF]
             rows = slice(HALF * h, HALF * h + HALF)
             drain = mask_ref[0, rows, cols].astype(F32) * evap_ref[0, rows, cols]
@@ -317,40 +397,11 @@
         src_ref[:, cols] = jnp.concatenate(sources, axis=0).astype(BF)
         return carry
 
-    lax.fori_loop(0, nblocks, forward, 0)
-    gath_f[own_rows, :] = src_ref[...]
-    source_copies = gather_copies(1, src_ref, gath_f)
-    for copy in source_copies:
-        copy.start()
-
-    def along_first(left, gathered, cols):
-        both = nn(left, gathered[:, cols])
-        total = both[: NCLS * ROWS] + both[NCLS * ROWS :]
-        classes = clsrow_ref[:, cols]
-        result = total[:ROWS]
-        for c in range(1, NCLS):
-            result = jnp.where(classes == c, total[c * ROWS : (c + 1) * ROWS], result)
-        return result
-
-    for s in range(1, GROUP):
-        remote(
-            back_ref,
-            gath_b.at[pl.ds(pl.multiple_of(((member + GROUP - s) % GROUP) * ROWS, ROWS), ROWS)],
-            ag_ssem.at[0, s - 1],
-            ag_rsem.at[0, s - 1],
-            group_peer(s),
-        ).wait()
-    left_t = jnp.concatenate(
-        [invt_ref[n, c, own_rows, :] for n in range(2) for c in range(NCLS)], axis=0
-    )
-    wide_cols = min(512, side)
-
-    def adjoint(i, carry):
-        cols = pl.ds(pl.multiple_of(i * wide_cols, wide_cols), wide_cols)
-        sg_ref[:, cols] = along_first(left_t, gath_b, cols)
-        return carry
-
-    lax.fori_loop(0, side // wide_cols, adjoint, 0)
+    lax.fori_loop(0, nblocks // 2, forward, 0)
+    span_solve(0, back_ref, sg_ref)
+    lax.fori_loop(nblocks // 2, nblocks, forward, 0)
+    span_out(1, src_ref)
+    span_in(0, sg_ref)
 
     cacc_ref[...] = jnp.zeros_like(cacc_ref)
     macc_ref[...] = jnp.zeros_like(macc_ref)
@@ -360,24 +411,19 @@
         cols = pl.ds(pl.multiple_of(i * WIDTH, WIDTH), WIDTH)
         flux_sum = facc_ref[...]
         mixing = macc_ref[...]
+        flux_cots = TIME_STEP * sg_ref[:, cols].astype(F32)
         for h in range(2):
-            flux_cot = TIME_STEP * sg_ref[HALF * h : HALF * h + HALF, cols]
-            cots = []
+            firsts = []
             for r in range(HALF):
                 of = slice(r * HID, (r + 1) * HID)
-                row = jnp.broadcast_to(flux_cot[r : r + 1], (HID, WIDTH))
+                at_row = HALF * h + r
+                row = jnp.broadcast_to(flux_cots[at_row : at_row + 1], (HID, WIDTH))
                 flux_sum = flux_sum + sa_ref[h, of, cols].astype(F32) * row
-                second_cot = (fwc_ref[...] * row).astype(BF).astype(F32)
-                pre = (second_cot * d2_ref[h, of, cols]).astype(BF)
+                pre = (u_ref[h, of, cols].astype(F32) * row).astype(BF)
                 mixing = mixing + nt(a1_ref[h, of, cols], pre)
-                cots.append(pre)
-            firsts = []
-            for q in range(2):
-                first_cot = nn(bdb_ref[...], jnp.concatenate(cots[4 * q : 4 * q + 4], axis=0))
-                first_cot = first_cot.astype(BF).astype(F32)
-                firsts.append((first_cot * d1_ref[h, WIDTH * q : WIDTH * q + WIDTH, cols]).astype(BF))
+                firsts.append((v_ref[h, of, cols].astype(F32) * row).astype(BF))
             pre_first = jnp.concatenate(firsts, axis=0)
-            a1_ref[h, :, cols] = pre_first
+            v_ref[h, :, cols] = pre_first
             cacc_ref[...] += nt(pre_first, x_ref[h, :, cols])
         facc_ref[...] = flux_sum
         macc_ref[...] = mixing
@@ -423,10 +469,12 @@
     for copy in stage1:
         copy.start()
 
+    span_solve(1, src_ref, across_ref)
+
     def features_back(i, carry):
         cols = pl.ds(pl.multiple_of(i * WIDTH, WIDTH), WIDTH)
         for h in range(2):
-            tt_ref[h, :, cols] = nn(wct_ref[...], a1_ref[h, :, cols])
+            tt_ref[h, :, cols] = nn(wct_ref[...], v_ref[h, :, cols])
         return carry
 
     lax.fori_loop(0, nblocks, features_back, 0)
@@ -480,35 +528,19 @@
     rim_up.start()
     rim_down.start()
 
-    for s in range(1, GROUP):
-        remote(
-            src_ref,
-            gath_f.at[pl.ds(pl.multiple_of(((member + GROUP - s) % GROUP) * ROWS, ROWS), ROWS)],
-            ag_ssem.at[1, s - 1],
-            ag_rsem.at[1, s - 1],
-            group_peer(s),
-        ).wait()
-    left_f = jnp.concatenate(
-        [
-            half[pl.ds(pl.multiple_of(c * SPAN + member * ROWS, ROWS), ROWS), :]
-            for half in (invhi_ref, invlo_ref)
-            for c in range(NCLS)
-        ],
-        axis=0,
-    )
-    pieces = []
-    for i in range(side // wide_cols):
-        across = along_first(left_f, gath_f, slice(i * wide_cols, (i + 1) * wide_cols))
-        for k in range(wide_cols // SPAN):
-            pieces.append(across[:, k * SPAN : (k + 1) * SPAN])
-    l_hi, l_lo = split2(jnp.concatenate(pieces, axis=0))
-    f_hi = invhi_ref[...]
-    products = nt(l_hi, f_hi) + nt(l_lo, f_hi) + nt(l_hi, invlo_ref[...])
+    span_in(1, across_ref)
+    pieces = [across_ref[:, k * SPAN : (k + 1) * SPAN] for k in range(nspan)]
+    lines = jnp.concatenate(pieces, axis=0)
+    f_hi = invs_ref[1, 0].reshape(NCLS * SPAN, SPAN)
+    f_lo = invs_ref[1, 1].reshape(NCLS * SPAN, SPAN)
+    products = nt(lines, f_hi) + nt(lines, f_lo)
 
     def store_final(k, value):
         final_ref[0, :, k * SPAN : (k + 1) * SPAN] = value
 
     span_select(products, scls_ref, store_final)
+    final_out = pltpu.make_async_copy(final_ref, final_hbm, out_sem.at[0])
+    final_out.start()
 
     finish(1, p2_ref, z_at, q1_ref, z_peer)
     q2_ref[...] = summed(p2_ref)
@@ -522,7 +554,9 @@
         tot_ref[c, ROWS : ROWS + 1, :] += jnp.where(sp < nsp - 1, rim_r[1, c : c + 1, :], 0.0)
     cot0 = tot_ref[0, 1 : ROWS + 1, :].astype(BF).astype(F32)
     cot1 = tot_ref[1, 1 : ROWS + 1, :].astype(BF).astype(F32)
-    grad_ref[0] = sg_ref[...] + cot0 + 2.0 * film_ref[0] * cot1
+    grad_ref[0] = sg_ref[...].astype(F32) + cot0 + 2.0 * film_ref[0] * cot1
+    grad_out = pltpu.make_async_copy(grad_ref, grad_hbm, out_sem.at[1])
+    grad_out.start()
 
     finish(2, p3_ref, y_at, q2_ref, y_peer)
     q3_ref[...] = summed(p3_ref)
@@ -530,7 +564,18 @@
     begin(3, p4_ref, j_at, q3_ref, corner_peer)
     finish(3, p4_ref, j_at, q3_ref, corner_peer)
     scale = 1.0 / math.sqrt(DYHI * DCORE * side * side)
-    result = p4_ref[...].reshape(HID, 2 * HID) * scale
+    gsum_ref[...] = p4_ref[...].reshape(HID, 2 * HID) * scale
+    gsum_out = pltpu.make_async_copy(gsum_ref, gsum_hbm, out_sem.at[2])
+    gsum_out.start()
+    final_out.wait()
+    grad_out.wait()
+    gsum_out.wait()
+
+
+def hand_out(final_in, grad_in, gsum_in, final_ref, grad_ref, convg_ref, mixg_ref, fluxg_ref):
+    final_ref[...] = final_in[...]
+    grad_ref[...] = grad_in[...]
+    result = gsum_in[...]
     mixg_ref[...] = result[:, :HID]
     other = pltpu.roll(result, HID, axis=1)[:, :HID]
     for a in range(3):
@@ -544,42 +589,56 @@
     side = film.shape[2]
     rows = film.shape[1]
     vmem = pl.BlockSpec(memory_space=pltpu.VMEM)
-    outs = pl.pallas_call(
+    hbm = pl.BlockSpec(memory_space=pl.ANY)
+    args = (
+        film,
+        evap,
+        mask,
+        jnp.swapaxes(fcls, 1, 2),
+        scls,
+        inv,
+        convw,
+        mixw,
+        fluxw.reshape(1, HID),
+        cot,
+    )
+    chunk = side // GROUP
+    tall = HALF * HID
+    slab = jax.ShapeDtypeStruct(film.shape, F32)
+    block = jax.ShapeDtypeStruct((HID, 2 * HID), F32)
+    final, grad, gsum = pl.pallas_call(
         kernel,
-        out_shape=(
-            jax.ShapeDtypeStruct(film.shape, F32),
-            jax.ShapeDtypeStruct(film.shape, F32),
-            jax.ShapeDtypeStruct(convw.shape, F32),
-            jax.ShapeDtypeStruct(mixw.shape, F32),
-            jax.ShapeDtypeStruct((1, HID), F32),
-        ),
-        in_specs=[vmem] * 10,
-        out_specs=(vmem,) * 5,
-        scratch_shapes=[
-            pltpu.VMEM((NCLS * SPAN, SPAN), BF),
-            pltpu.VMEM((NCLS * SPAN, SPAN), BF),
-            pltpu.VMEM((2, NCLS, SPAN, SPAN), BF),
-            pltpu.VMEM((SPAN, side), BF),
-            pltpu.VMEM((SPAN, side), BF),
+        out_shape=(slab, slab, block),
+        in_specs=[hbm] * 10,
+        out_specs=(hbm,) * 3,
+        scratch_shapes=[pltpu.VMEM(a.shape, a.dtype) for a in args]
+        + [
+            pltpu.VMEM(film.shape, F32),
+            pltpu.VMEM(film.shape, F32),
+            pltpu.VMEM((HID, 2 * HID), F32),
+            pltpu.VMEM((2, 2, NCLS, SPAN, SPAN), BF),
+            pltpu.VMEM((2, SPAN, chunk), BF),
+            pltpu.VMEM((2, SPAN, chunk), BF),
             pltpu.VMEM((2, CIN, side), F32),
             pltpu.VMEM((2, CIN, side), F32),
             pltpu.VMEM((CIN, 24, side), F32),
             pltpu.VMEM((2, PIECES * 16, side), BF),
-            pltpu.VMEM((HALF * HID, WIDTH), BF),
-            pltpu.VMEM((96, HALF * HID), BF),
+            pltpu.VMEM((tall, WIDTH), BF),
+            pltpu.VMEM((96, tall), BF),
             pltpu.VMEM((WIDTH, WIDTH), BF),
             pltpu.VMEM((WIDTH, WIDTH), BF),
-            pltpu.VMEM((16, HALF * HID), BF),
-            pltpu.VMEM((HID, WIDTH), F32),
-            pltpu.VMEM((16, side), F32),
-            pltpu.VMEM((2, HALF * HID, side), BF),
-            pltpu.VMEM((2, HALF * HID, side), F32),
-            pltpu.VMEM((2, HALF * HID, side), BF),
-            pltpu.VMEM((2, HALF * HID, side), F32),
+            pltpu.VMEM((16, tall), BF),
+            pltpu.VMEM((WIDTH, WIDTH), F32),
+            pltpu.VMEM((2, tall, side), BF),
+            pltpu.VMEM((2, tall, WIDTH), F32),
+            pltpu.VMEM((2, tall, side), BF),
+            pltpu.VMEM((2, tall, side), BF),
+            pltpu.VMEM((2, tall, side), BF),
             pltpu.VMEM((rows, side), BF),
             pltpu.VMEM((rows, side), BF),
-            pltpu.VMEM((rows, side), F32),
-            pltpu.VMEM((HALF * HID, PIECES * 16), F32),
+            pltpu.VMEM((rows, side), BF),
+            pltpu.VMEM((rows, side), BF),
+            pltpu.VMEM((tall, PIECES * 16), F32),
             pltpu.VMEM((HID, HID), F32),
             pltpu.VMEM((HID, WIDTH), F32),
             pltpu.VMEM((2, 96, side), F32),
@@ -595,8 +654,10 @@
             pltpu.VMEM((8, 8, 2 * HID), F32),
             pltpu.VMEM((8, 2 * HID), F32),
             pltpu.VMEM((8, 8, 2 * HID), F32),
-            pltpu.SemaphoreType.DMA((2, 7)),
-            pltpu.SemaphoreType.DMA((2, 7)),
+            pltpu.SemaphoreType.DMA((10,)),
+            pltpu.SemaphoreType.DMA((3,)),
+            pltpu.SemaphoreType.DMA((4, 7)),
+            pltpu.SemaphoreType.DMA((4, 7)),
             pltpu.SemaphoreType.DMA((4,)),
             pltpu.SemaphoreType.DMA((4,)),
             pltpu.SemaphoreType.DMA((4, 7)),
@@ -605,7 +666,19 @@
         compiler_params=pltpu.CompilerParams(
             collective_id=0, has_side_effects=True, vmem_limit_bytes=60 * 1024 * 1024
         ),
-    )(film, evap, mask, fcls, scls, inv, convw, mixw, fluxw.reshape(1, HID), cot)
+    )(*args)
+    outs = pl.pallas_call(
+        hand_out,
+        out_shape=(
+            slab,
+            slab,
+            jax.ShapeDtypeStruct(convw.shape, F32),
+            jax.ShapeDtypeStruct(mixw.shape, F32),
+            jax.ShapeDtypeStruct((1, HID), F32),
+        ),
+        in_specs=[vmem] * 3,
+        out_specs=(vmem,) * 5,
+    )(final, grad, gsum)
     return outs[0], outs[1], outs[2], outs[3], outs[4].reshape(HID)
 
 

time: 63.4 us -> 56.6 us (0.89)
  local copies, waits for them, and re-layouts: 6.48 us -> 0 us
    unnamed x14 -> x0, local copies, waits for them, and re-layouts: 6.48 us -> none
    pallas_call x1 -> x2, Pallas kernels: 55.9 us -> 55.8 us  [the longest x1 54.2 us: on_device(): pl.pallas_call(kernel, out_shape=(slab, slab, block), in_specs=[hbm] * 10...]
where the time goes in v2:
time: 56.6 us; the launch traced here: 56.5 us
  Pallas kernels  55.8 us (99%)
  between operations  0.64 us (1%)
    pallas_call x1, Pallas kernels, on_device(): pl.pallas_call(kernel, out_shape=(slab, slab, block), in_specs=[hbm] * 10...  54.2 us
    pallas_call x1, Pallas kernels, on_device(): pl.pallas_call(hand_out, out_shape=(slab, slab, jax.ShapeDtypeStruct(conv...  1.7 us

profile of v2, /device:TPU:1, one launch (start us, length us, event | category | flops | bytes accessed | tf_op | source)
XLA Modules:
  0.0 56.5 jit_solution(8567338767400298017)
XLA Ops:
  0.6 54.2 %shard_map.137 = (f32[1,16,2048]{2,1,0:T(8,128)}, f32[1,16,2048]{2,1,0:T(8,128)}, f32[64,128]{1,0:T(8,128)}) custom-call(f32[1,16,2048]{2,1,0:T(8,128)} %film_hbm.1, f32[1,16,2048]{2,1,0:T(8,128)} %evap_hbm.1, s32[1,16,2048]{2,1,0:T(8,128)} %mask_hbm.1, s32[1,16,2048]{2,1,0:T(8,128)} %bitcast.3, s32[1,16,16]{2,1,0:T(8,128)} %scls_hbm.1, ...), custom_call_target="tpu_custom_call" | custom-call | tf_op jit(solution)/shard_map/pallas_call | solution.py:609
  54.8 1.7 %shard_map.138 = (f32[1,16,2048]{2,1,0:T(8,128)}, f32[1,16,2048]{2,1,0:T(8,128)}, f32[3,3,4,64]{3,2,1,0:T(4,128)}, f32[64,64]{1,0:T(8,128)}, f32[1,64]{1,0:T(1,128)}) custom-call(f32[1,16,2048]{2,1,0:T(8,128)} %get-tuple-element.13.final_in, f32[1,16,2048]{2,1,0:T(8,128)} %get-tuple-element.14.grad_in, f32[64,128]{1,0:T(8,128)} %get-tuple-element.15.gsum_in), custom_call_target="tpu_custom_call" | custom-call | tf_op jit(solution)/shard_map/pallas_call | solution.py:670

commit v3 on v2

--- a/solution.py
+++ b/solution.py
@@ -41,6 +41,31 @@
     rest = v - hi.astype(F32)
     mid = rest.astype(BF)
     return hi, mid, (rest - mid.astype(F32)).astype(BF)
+
+
+def mod(a, n):
+    return lax.rem(a, jnp.int32(n))
+
+
+def div(a, n):
+    return lax.div(a, jnp.int32(n))
+
+
+def shift_of(group, r):
+    return r if group == 0 or r < HALF // 2 else r + HALF // 2
+
+
+def row_of(group, r):
+    if group == 0:
+        return r + HALF // 2
+    return r if r < HALF // 2 else r + HALF
+
+
+def group_rows(values, group):
+    quarter = HALF // 2
+    if group == 0:
+        return values[quarter : quarter + HALF]
+    return jnp.concatenate([values[:quarter], values[quarter + HALF :]], axis=0)
 
 
 def iota(shape, dim):
@@ -106,6 +131,8 @@
     sa_ref,
     u_ref,
     v_ref,
+    la_ref,
+    srcf_ref,
     src_ref,
     back_ref,
     sg_ref,
@@ -152,46 +179,45 @@
             )
         )
     ]
-    for copy in inputs:
+    for copy in inputs[:3]:
         copy.start()
     side = film_ref.shape[2]
     nblocks = side // WIDTH
     sp = lax.axis_index("sp")
     rep = lax.axis_index("rep")
     nsp = DYLO * DZ * DX
-    x_at = sp % DX
-    z_at = (sp // DX) % DZ
-    ylo_at = sp // (DX * DZ)
-    yhi_at = rep // DCORE
-    core_at = rep % DCORE
+    x_at = mod(sp, DX)
+    z_at = mod(div(sp, DX), DZ)
+    ylo_at = div(sp, DX * DZ)
+    yhi_at = div(rep, DCORE)
+    core_at = mod(rep, DCORE)
     y_at = yhi_at * DYLO + ylo_at
-    member = sp % GROUP
+    member = mod(sp, GROUP)
     first = sp - member
 
     def at(r, s):
         return {"rep": r, "sp": s}
 
-    up = (sp + nsp - 1) % nsp
-    down = (sp + 1) % nsp
+    up = mod(sp + nsp - 1, nsp)
+    down = mod(sp + 1, nsp)
 
     def group_peer(s):
-        return at(rep, first + (member + s) % GROUP)
+        return at(rep, first + mod(member + s, GROUP))
 
     j_at = core_at * DX + x_at
 
     def corner_peer(s):
-        other = (j_at + s) % (DCORE * DX)
-        return at(yhi_at * DCORE + other // DX, sp - x_at + other % DX)
+        other = mod(j_at + s, DCORE * DX)
+        return at(yhi_at * DCORE + div(other, DX), sp - x_at + mod(other, DX))
 
     def z_peer(s):
-        other = (z_at + s) % DZ
-        return at(rep, (ylo_at * DZ + other) * DX + x_at)
+        return at(rep, sp + (mod(z_at + s, DZ) - z_at) * DX)
 
     def y_peer(s):
-        other = (y_at + s) % (DYHI * DYLO)
+        other = mod(y_at + s, DYHI * DYLO)
         return at(
-            (other // DYLO) * DCORE + core_at,
-            ((other % DYLO) * DZ + z_at) * DX + x_at,
+            div(other, DYLO) * DCORE + core_at,
+            sp + (mod(other, DYLO) - ylo_at) * DX * DZ,
         )
 
     barrier = pltpu.get_barrier_semaphore()
@@ -200,6 +226,8 @@
         peers += [group_peer(s), corner_peer(s), z_peer(s), y_peer(s)]
     for peer in peers:
         pl.semaphore_signal(barrier, inc=1, device_id=peer, device_id_type=MESH)
+    for copy in inputs[3:]:
+        copy.start()
 
     def remote(src, dst, ssem, rsem, peer):
         return pltpu.make_async_remote_copy(
@@ -244,32 +272,29 @@
     def rows_of(n):
         return pl.ds(pl.multiple_of(n * ROWS, ROWS), ROWS)
 
-    def from_peer(s):
-        return (member + GROUP - s) % GROUP
-
     def span_out(which, field):
         recv_ref[which, own_rows, :] = field[:, columns_of(member)]
         for s in range(1, GROUP):
             remote(
-                field.at[:, columns_of((member + s) % GROUP)],
+                field.at[:, columns_of(mod(member + s, GROUP))],
                 recv_ref.at[which, own_rows],
-                ag_ssem.at[2 * which, s - 1],
-                ag_rsem.at[2 * which, s - 1],
+                ag_ssem.at[2 * which],
+                ag_rsem.at[2 * which],
                 group_peer(s),
             ).start()
 
     def span_solve(which, field, result):
-        for s in range(1, GROUP):
-            remote(
-                field.at[:, columns_of((member + s) % GROUP)],
-                recv_ref.at[which, rows_of(from_peer(s))],
-                ag_ssem.at[2 * which, s - 1],
-                ag_rsem.at[2 * which, s - 1],
-                group_peer(s),
-            ).wait()
+        others = GROUP - 1
+        remote(
+            field.at[:, pl.ds(0, others * chunk)],
+            recv_ref.at[which, pl.ds(0, others * ROWS)],
+            ag_ssem.at[2 * which],
+            ag_rsem.at[2 * which],
+            group_peer(1),
+        ).wait()
         values = recv_ref[which]
         line_cls = fcls_ref[0, :, columns_of(member)]
-        own_span = iota(line_cls.shape, 0) == sp // GROUP
+        own_span = iota(line_cls.shape, 0) == div(sp, GROUP)
         classes = jnp.sum(jnp.where(own_span, line_cls, 0), axis=0, keepdims=True)
         solved = None
         for c in range(NCLS):
@@ -279,22 +304,22 @@
         result[:, columns_of(member)] = mid_ref[which, own_rows, :]
         for s in range(1, GROUP):
             remote(
-                mid_ref.at[which, rows_of((member + s) % GROUP)],
+                mid_ref.at[which, rows_of(mod(member + s, GROUP))],
                 result.at[:, columns_of(member)],
-                ag_ssem.at[2 * which + 1, s - 1],
-                ag_rsem.at[2 * which + 1, s - 1],
+                ag_ssem.at[2 * which + 1],
+                ag_rsem.at[2 * which + 1],
                 group_peer(s),
             ).start()
 
     def span_in(which, result):
-        for s in range(1, GROUP):
-            remote(
-                mid_ref.at[which, rows_of((member + s) % GROUP)],
-                result.at[:, columns_of(from_peer(s))],
-                ag_ssem.at[2 * which + 1, s - 1],
-                ag_rsem.at[2 * which + 1, s - 1],
-                group_peer(s),
-            ).wait()
+        others = GROUP - 1
+        remote(
+            mid_ref.at[which, pl.ds(0, others * ROWS)],
+            result.at[:, pl.ds(0, others * chunk)],
+            ag_ssem.at[2 * which + 1],
+            ag_rsem.at[2 * which + 1],
+            group_peer(1),
+        ).wait()
 
     for copy in inputs[3:]:
         copy.wait()
@@ -308,15 +333,6 @@
         padf_ref[c, ROWS + 2 :, :] = jnp.zeros((6, side), F32)
         halo_s[0, c : c + 1, :] = feature[0:1]
         halo_s[1, c : c + 1, :] = feature[ROWS - 1 :]
-
-    pl.semaphore_wait(barrier, len(peers))
-
-    halo_up = remote(halo_s.at[0], halo_r.at[1], nb_ssem.at[0], nb_rsem.at[0], at(rep, up))
-    halo_down = remote(halo_s.at[1], halo_r.at[0], nb_ssem.at[1], nb_rsem.at[1], at(rep, down))
-    halo_up.start()
-    halo_down.start()
-
-    span_out(0, back_ref)
 
     w36_ref[...] = jnp.zeros_like(w36_ref)
     for a in range(3):
@@ -331,11 +347,13 @@
     wanted = (tap_row * 3 + piece % 3) * CIN + piece // 3
     pick = (k_at == wanted) & (tap_row < 3) & (piece < PIECES)
     band0 = nn(w_t, onehot(pick))
-    band = jnp.concatenate(
-        [band0] + [pltpu.roll(band0, r, axis=1) for r in range(1, HALF)], axis=0
-    )
-    wb_ref[...] = band.astype(BF)
-    wct_ref[...] = band[:, :SPAN].T[:96].astype(BF)
+    for g in range(2):
+        shifts = [shift_of(g, r) for r in range(HALF)]
+        band = jnp.concatenate(
+            [band0 if n == 0 else pltpu.roll(band0, n, axis=1) for n in shifts], axis=0
+        )
+        wb_ref[g] = band.astype(BF)
+        wct_ref[g] = band[:, :SPAN].T[:96].astype(BF)
     mix = mixw_ref[...]
     tile4 = onehot(iota((HID, WIDTH), 1) % HID == iota((HID, WIDTH), 0))
     wide = nn(mix, tile4)
@@ -355,51 +373,102 @@
     )
     fwc_ref[...] = jnp.concatenate([jnp.broadcast_to(fw_col, (HID, WIDTH))] * 4, axis=0)
 
-    halo_up.wait()
-    halo_down.wait()
+    lane = iota((24, side), 1)
+
+    def build_pieces(g):
+        for c in range(CIN):
+            middle = padf_ref[c]
+            left = jnp.where(lane == 0, 0.0, pltpu.roll(middle, 1, axis=1))
+            right = jnp.where(lane == side - 1, 0.0, pltpu.roll(middle, side - 1, axis=1))
+            for b, values in enumerate((left, middle, right)):
+                s = (c * 3 + b) * 16
+                if g == 0:
+                    piece = values[4:20]
+                else:
+                    piece = jnp.concatenate([values[0:8], values[12:20]], axis=0)
+                x_ref[g, s : s + 16, :] = piece.astype(BF)
+
+    def forward(g):
+        def body(i, carry):
+            def cols_at(n):
+                start = pl.multiple_of(i * (2 * WIDTH) + n * WIDTH, WIDTH)
+                return pl.ds(start, WIDTH)
+
+            def first_layer(n):
+                cols = cols_at(n)
+                t1 = jnp.tanh(nn(wb_ref[g, :, : PIECES * 16], x_ref[g, :, cols]))
+                a1 = t1.astype(BF)
+                a1_ref[g, :, cols] = a1
+                la_ref[n] = a1
+                d1_ref[n] = 1.0 - t1 * t1
+
+            factors = {}
+
+            def second_layer(n, q):
+                of = slice(q * WIDTH, (q + 1) * WIDTH)
+                cols = cols_at(n)
+                t2 = jnp.tanh(nn(bdf_ref[...], la_ref[n, of, :]))
+                sa_ref[g, of, cols] = t2.astype(BF)
+                u = (fwc_ref[...] * (1.0 - t2 * t2)).astype(BF)
+                u_ref[g, of, cols] = u
+                factors[n, q] = (u, t2.astype(BF))
+
+            def combine(n, q):
+                of = slice(q * WIDTH, (q + 1) * WIDTH)
+                v = d1_ref[n, of, :] * nn(bdb_ref[...], factors[n, q][0])
+                v_ref[g, of, cols_at(n)] = v.astype(BF)
+
+            def sources(n):
+                cols = cols_at(n)
+                sa = jnp.concatenate([factors[n, 0][1], factors[n, 1][1]], axis=0)
+                flux = nn(fwb_ref[...], sa)[:HALF]
+                drain = mask_ref[0, :, cols].astype(F32) * evap_ref[0, :, cols]
+                rest = film_ref[0, :, cols] - TIME_STEP * drain
+                source = group_rows(rest, g) + TIME_STEP * flux
+                quarter = HALF // 2
+                if g == 0:
+                    srcf_ref[quarter : quarter + HALF, cols] = source
+                else:
+                    srcf_ref[0:quarter, cols] = source[:quarter]
+                    srcf_ref[quarter + HALF :, cols] = source[quarter:]
+
+            first_layer(0)
+            second_layer(0, 0)
+            first_layer(1)
+            second_layer(0, 1)
+            combine(0, 0)
+            second_layer(1, 0)
+            combine(0, 1)
+            sources(0)
+            second_layer(1, 1)
+            combine(1, 0)
+            combine(1, 1)
+            sources(1)
+            return carry
+
+        return body
+
+    pairs = nblocks // 2
+    build_pieces(0)
+    lax.fori_loop(0, 1, forward(0), 0)
+
+    pl.semaphore_wait(barrier, len(peers))
+    remote(halo_s.at[0], halo_r.at[1], nb_ssem.at[0], nb_rsem.at[0], at(rep, up)).start()
+    remote(halo_s.at[1], halo_r.at[0], nb_ssem.at[0], nb_rsem.at[0], at(rep, down)).start()
+    span_out(0, back_ref)
+
+    lax.fori_loop(1, pairs, forward(0), 0)
+
+    remote(halo_s, halo_r, nb_ssem.at[0], nb_rsem.at[0], at(rep, up)).wait()
     for c in range(CIN):
         padf_ref[c, 0:1, :] = jnp.where(sp > 0, halo_r[0, c : c + 1, :], 0.0)
         padf_ref[c, ROWS + 1 : ROWS + 2, :] = jnp.where(
             sp < nsp - 1, halo_r[1, c : c + 1, :], 0.0
         )
-    lane = iota((24, side), 1)
-    for c in range(CIN):
-        middle = padf_ref[c]
-        left = jnp.where(lane == 0, 0.0, pltpu.roll(middle, 1, axis=1))
-        right = jnp.where(lane == side - 1, 0.0, pltpu.roll(middle, side - 1, axis=1))
-        for b, values in enumerate((left, middle, right)):
-            s = (c * 3 + b) * 16
-            for h in range(2):
-                x_ref[h, s : s + 16, :] = values[HALF * h : HALF * h + 16].astype(BF)
-
-    def forward(i, carry):
-        cols = pl.ds(pl.multiple_of(i * WIDTH, WIDTH), WIDTH)
-        sources = []
-        for h in range(2):
-            t1 = jnp.tanh(nn(wb_ref[:, : PIECES * 16], x_ref[h, :, cols]))
-            a1 = t1.astype(BF)
-            a1_ref[h, :, cols] = a1
-            d1_ref[h] = 1.0 - t1 * t1
-            actives = []
-            for q in range(2):
-                of = slice(q * WIDTH, (q + 1) * WIDTH)
-                t2 = jnp.tanh(nn(bdf_ref[...], a1[of]))
-                actives.append(t2.astype(BF))
-                u = (fwc_ref[...] * (1.0 - t2 * t2)).astype(BF)
-                u_ref[h, of, cols] = u
-                v_ref[h, of, cols] = (d1_ref[h, of, :] * nn(bdb_ref[...], u)).astype(BF)
-            sa = jnp.concatenate(actives, axis=0)
-            sa_ref[h, :, cols] = sa
-            flux = nn(fwb_ref[...], sa)[:HALF]
-            rows = slice(HALF * h, HALF * h + HALF)
-            drain = mask_ref[0, rows, cols].astype(F32) * evap_ref[0, rows, cols]
-            sources.append(film_ref[0, rows, cols] + TIME_STEP * (flux - drain))
-        src_ref[:, cols] = jnp.concatenate(sources, axis=0).astype(BF)
-        return carry
-
-    lax.fori_loop(0, nblocks // 2, forward, 0)
+    build_pieces(1)
     span_solve(0, back_ref, sg_ref)
-    lax.fori_loop(nblocks // 2, nblocks, forward, 0)
+    lax.fori_loop(0, pairs, forward(1), 0)
+    src_ref[...] = srcf_ref[...].astype(BF)
     span_out(1, src_ref)
     span_in(0, sg_ref)
 
@@ -409,46 +478,55 @@
 
     def backward(i, carry):
         cols = pl.ds(pl.multiple_of(i * WIDTH, WIDTH), WIDTH)
-        flux_sum = facc_ref[...]
         mixing = macc_ref[...]
         flux_cots = TIME_STEP * sg_ref[:, cols].astype(F32)
-        for h in range(2):
+        for g in range(2):
             firsts = []
             for r in range(HALF):
                 of = slice(r * HID, (r + 1) * HID)
-                at_row = HALF * h + r
-                row = jnp.broadcast_to(flux_cots[at_row : at_row + 1], (HID, WIDTH))
-                flux_sum = flux_sum + sa_ref[h, of, cols].astype(F32) * row
-                pre = (u_ref[h, of, cols].astype(F32) * row).astype(BF)
-                mixing = mixing + nt(a1_ref[h, of, cols], pre)
-                firsts.append((v_ref[h, of, cols].astype(F32) * row).astype(BF))
+                at_row = row_of(g, r)
+                row = jnp.broadcast_to(flux_cots[at_row : at_row + 1], (HID, WIDTH)).astype(BF)
+                mixing = mixing + nt(a1_ref[g, of, cols], u_ref[g, of, cols] * row)
+                firsts.append(v_ref[g, of, cols] * row)
             pre_first = jnp.concatenate(firsts, axis=0)
-            v_ref[h, :, cols] = pre_first
-            cacc_ref[...] += nt(pre_first, x_ref[h, :, cols])
-        facc_ref[...] = flux_sum
+            v_ref[g, :, cols] = pre_first
+            cots = group_rows(flux_cots, g).astype(BF)
+            facc_ref[...] += nt(cots, sa_ref[g, :, cols])
+            cacc_ref[g] += nt(pre_first, x_ref[g, :, cols])
         macc_ref[...] = mixing
         return carry
 
     lax.fori_loop(0, nblocks, backward, 0)
 
-    whole = jnp.concatenate(
-        [cacc_ref[...], jnp.zeros((HALF * HID, WIDTH - PIECES * 16), F32)], axis=1
-    )
-    taps = whole[:HID]
-    for r in range(1, HALF):
-        taps = taps + pltpu.roll(whole[r * HID : (r + 1) * HID], WIDTH - r, axis=1)
+    rolled = {}
+    for g in range(2):
+        for r in range(HALF):
+            n = shift_of(g, r)
+            term = cacc_ref[g, r * HID : (r + 1) * HID]
+            rolled[n] = term if n not in rolled else rolled[n] + term
+    taps = jnp.zeros((HID, WIDTH), F32)
+    spare = jnp.zeros((HID, WIDTH - PIECES * 16), F32)
+    for n, term in rolled.items():
+        whole = jnp.concatenate([term, spare], axis=1)
+        taps = taps + (whole if n == 0 else pltpu.roll(whole, WIDTH - n, axis=1))
     k_at = iota((HID, WIDTH), 0)
     col = iota((HID, WIDTH), 1)
     piece = col // 16
     tap_row = col % 16
     wanted = (tap_row * 3 + piece % 3) * CIN + piece // 3
     pick = onehot((k_at == wanted) & (tap_row < 3) & (piece < PIECES))
-    ones_row = onehot(k_at == 9 * CIN)
     low = jnp.zeros((HID, WIDTH), BF)
     right = jnp.zeros((HID, 2 * HID), F32)
-    for t, f in zip(split3(taps), split3(facc_ref[...])):
+    for t in split3(taps):
         right = right + nt(pick, jnp.concatenate([low, t], axis=0))
-        right = right + nt(ones_row, jnp.concatenate([low, f], axis=0))
+    tall = HALF * HID
+    fold = onehot(mod(iota((tall, 2 * HID), 0), HID) + HID == iota((tall, 2 * HID), 1))
+    mine = div(iota((HALF, tall), 1), HID) == iota((HALF, tall), 0)
+    flux_rows = jnp.zeros((HALF, 2 * HID), F32)
+    for f in split3(jnp.where(mine, facc_ref[...], 0.0)):
+        flux_rows = flux_rows + nn(f, fold)
+    flux_row = jnp.sum(flux_rows, axis=0, keepdims=True)
+    right = right + jnp.where(iota((HID, 2 * HID), 0) == 9 * CIN, flux_row, 0.0)
     g_ref[...] = right
     g_ref[:, 0:HID] = macc_ref[...]
 
@@ -456,13 +534,13 @@
     p1_ref[j_at] = g_ref[own_block, :]
     stage1 = []
     for s in range(1, 8):
-        other = (j_at + s) % 8
+        other = mod(j_at + s, 8)
         stage1.append(
             remote(
                 g_ref.at[pl.ds(pl.multiple_of(other * 8, 8), 8)],
                 p1_ref.at[j_at],
-                ar_ssem.at[0, s - 1],
-                ar_rsem.at[0, s - 1],
+                ar_ssem.at[0],
+                ar_rsem.at[0],
                 corner_peer(s),
             )
         )
@@ -474,28 +552,27 @@
     def features_back(i, carry):
         cols = pl.ds(pl.multiple_of(i * WIDTH, WIDTH), WIDTH)
         for h in range(2):
-            tt_ref[h, :, cols] = nn(wct_ref[...], v_ref[h, :, cols])
+            tt_ref[h, :, cols] = nn(wct_ref[h], v_ref[h, :, cols])
         return carry
 
     lax.fori_loop(0, nblocks, features_back, 0)
 
-    def finish(stage, slots, at_index, source, send_peer):
-        for s in range(1, 8):
-            remote(
-                source,
-                slots.at[(at_index + 8 - s) % 8],
-                ar_ssem.at[stage, s - 1],
-                ar_rsem.at[stage, s - 1],
-                send_peer(s),
-            ).wait()
+    def finish(stage, slots, send_peer):
+        remote(
+            slots.at[pl.ds(0, 7)],
+            slots.at[pl.ds(0, 7)],
+            ar_ssem.at[stage],
+            ar_rsem.at[stage],
+            send_peer(1),
+        ).wait()
 
     def begin(stage, slots, at_index, source, send_peer):
         for s in range(1, 8):
             remote(
                 source,
                 slots.at[at_index],
-                ar_ssem.at[stage, s - 1],
-                ar_rsem.at[stage, s - 1],
+                ar_ssem.at[stage],
+                ar_rsem.at[stage],
                 send_peer(s),
             ).start()
 
@@ -505,7 +582,7 @@
             total = total + slots[n]
         return total
 
-    finish(0, p1_ref, j_at, g_ref.at[own_block], corner_peer)
+    finish(0, p1_ref, corner_peer)
     q1_ref[...] = summed(p1_ref)
     p2_ref[z_at] = q1_ref[...]
     begin(1, p2_ref, z_at, q1_ref, z_peer)
@@ -518,15 +595,14 @@
             left = jnp.where(lane == side - 1, 0.0, pltpu.roll(tt_ref[h, s : s + 16, :], side - 1, axis=1))
             right = jnp.where(lane == 0, 0.0, pltpu.roll(tt_ref[h, s + 32 : s + 48, :], 1, axis=1))
             parts.append(left + tt_ref[h, s + 16 : s + 32, :] + right)
-        tot_ref[c, 0:8, :] = parts[0][0:8]
-        tot_ref[c, 8:16, :] = parts[0][8:16] + parts[1][0:8]
-        tot_ref[c, 16:24, :] = parts[1][8:16]
-        rim_s[0, c : c + 1, :] = parts[0][0:1]
-        rim_s[1, c : c + 1, :] = parts[1][9:10]
-    rim_up = remote(rim_s.at[0], rim_r.at[1], nb_ssem.at[2], nb_rsem.at[2], at(rep, up))
-    rim_down = remote(rim_s.at[1], rim_r.at[0], nb_ssem.at[3], nb_rsem.at[3], at(rep, down))
-    rim_up.start()
-    rim_down.start()
+        tot_ref[c, 0:8, :] = parts[1][0:8]
+        tot_ref[c, 8:12, :] = jnp.zeros((4, side), F32)
+        tot_ref[c, 12:20, :] = parts[1][8:16]
+        tot_ref[c, 4:20, :] += parts[0]
+        rim_s[0, c : c + 1, :] = parts[1][0:1]
+        rim_s[1, c : c + 1, :] = parts[1][13:14]
+    remote(rim_s.at[0], rim_r.at[1], nb_ssem.at[1], nb_rsem.at[1], at(rep, up)).start()
+    remote(rim_s.at[1], rim_r.at[0], nb_ssem.at[1], nb_rsem.at[1], at(rep, down)).start()
 
     span_in(1, across_ref)
     pieces = [across_ref[:, k * SPAN : (k + 1) * SPAN] for k in range(nspan)]
@@ -542,13 +618,12 @@
     final_out = pltpu.make_async_copy(final_ref, final_hbm, out_sem.at[0])
     final_out.start()
 
-    finish(1, p2_ref, z_at, q1_ref, z_peer)
+    finish(1, p2_ref, z_peer)
     q2_ref[...] = summed(p2_ref)
     p3_ref[y_at] = q2_ref[...]
     begin(2, p3_ref, y_at, q2_ref, y_peer)
 
-    rim_up.wait()
-    rim_down.wait()
+    remote(rim_s, rim_r, nb_ssem.at[1], nb_rsem.at[1], at(rep, up)).wait()
     for c in range(2):
         tot_ref[c, 1:2, :] += jnp.where(sp > 0, rim_r[0, c : c + 1, :], 0.0)
         tot_ref[c, ROWS : ROWS + 1, :] += jnp.where(sp < nsp - 1, rim_r[1, c : c + 1, :], 0.0)
@@ -558,11 +633,11 @@
     grad_out = pltpu.make_async_copy(grad_ref, grad_hbm, out_sem.at[1])
     grad_out.start()
 
-    finish(2, p3_ref, y_at, q2_ref, y_peer)
+    finish(2, p3_ref, y_peer)
     q3_ref[...] = summed(p3_ref)
     p4_ref[j_at] = q3_ref[...]
     begin(3, p4_ref, j_at, q3_ref, corner_peer)
-    finish(3, p4_ref, j_at, q3_ref, corner_peer)
+    finish(3, p4_ref, corner_peer)
     scale = 1.0 / math.sqrt(DYHI * DCORE * side * side)
     gsum_ref[...] = p4_ref[...].reshape(HID, 2 * HID) * scale
     gsum_out = pltpu.make_async_copy(gsum_ref, gsum_hbm, out_sem.at[2])
@@ -589,7 +664,8 @@
     side = film.shape[2]
     rows = film.shape[1]
     vmem = pl.BlockSpec(memory_space=pltpu.VMEM)
-    hbm = pl.BlockSpec(memory_space=pl.ANY)
+    hbm = pl.BlockSpec(memory_space=pltpu.HBM)
+    free = pl.BlockSpec(memory_space=pl.ANY)
     args = (
         film,
         evap,
@@ -602,6 +678,7 @@
         fluxw.reshape(1, HID),
         cot,
     )
+    args = tuple(pltpu.with_memory_space_constraint(a, pltpu.HBM) for a in args)
     chunk = side // GROUP
     tall = HALF * HID
     slab = jax.ShapeDtypeStruct(film.shape, F32)
@@ -610,7 +687,7 @@
         kernel,
         out_shape=(slab, slab, block),
         in_specs=[hbm] * 10,
-        out_specs=(hbm,) * 3,
+        out_specs=(free,) * 3,
         scratch_shapes=[pltpu.VMEM(a.shape, a.dtype) for a in args]
         + [
             pltpu.VMEM(film.shape, F32),
@@ -623,8 +700,8 @@
             pltpu.VMEM((2, CIN, side), F32),
             pltpu.VMEM((CIN, 24, side), F32),
             pltpu.VMEM((2, PIECES * 16, side), BF),
-            pltpu.VMEM((tall, WIDTH), BF),
-            pltpu.VMEM((96, tall), BF),
+            pltpu.VMEM((2, tall, WIDTH), BF),
+            pltpu.VMEM((2, 96, tall), BF),
             pltpu.VMEM((WIDTH, WIDTH), BF),
             pltpu.VMEM((WIDTH, WIDTH), BF),
             pltpu.VMEM((16, tall), BF),
@@ -634,13 +711,15 @@
             pltpu.VMEM((2, tall, side), BF),
             pltpu.VMEM((2, tall, side), BF),
             pltpu.VMEM((2, tall, side), BF),
+            pltpu.VMEM((2, tall, WIDTH), BF),
+            pltpu.VMEM((rows, side), F32),
             pltpu.VMEM((rows, side), BF),
             pltpu.VMEM((rows, side), BF),
             pltpu.VMEM((rows, side), BF),
             pltpu.VMEM((rows, side), BF),
-            pltpu.VMEM((tall, PIECES * 16), F32),
+            pltpu.VMEM((2, tall, PIECES * 16), F32),
             pltpu.VMEM((HID, HID), F32),
-            pltpu.VMEM((HID, WIDTH), F32),
+            pltpu.VMEM((HALF, tall), F32),
             pltpu.VMEM((2, 96, side), F32),
             pltpu.VMEM((2, 24, side), F32),
             pltpu.VMEM((2, 2, side), F32),
@@ -656,15 +735,15 @@
             pltpu.VMEM((8, 8, 2 * HID), F32),
             pltpu.SemaphoreType.DMA((10,)),
             pltpu.SemaphoreType.DMA((3,)),
-            pltpu.SemaphoreType.DMA((4, 7)),
-            pltpu.SemaphoreType.DMA((4, 7)),
             pltpu.SemaphoreType.DMA((4,)),
             pltpu.SemaphoreType.DMA((4,)),
-            pltpu.SemaphoreType.DMA((4, 7)),
-            pltpu.SemaphoreType.DMA((4, 7)),
+            pltpu.SemaphoreType.DMA((2,)),
+            pltpu.SemaphoreType.DMA((2,)),
+            pltpu.SemaphoreType.DMA((4,)),
+            pltpu.SemaphoreType.DMA((4,)),
         ],
         compiler_params=pltpu.CompilerParams(
-            collective_id=0, has_side_effects=True, vmem_limit_bytes=60 * 1024 * 1024
+            collective_id=0, has_side_effects=True, vmem_limit_bytes=48 * 1024 * 1024
         ),
     )(*args)
     outs = pl.pallas_call(
@@ -678,6 +757,7 @@
         ),
         in_specs=[vmem] * 3,
         out_specs=(vmem,) * 5,
+        compiler_params=pltpu.CompilerParams(vmem_limit_bytes=4 * 1024 * 1024),
     )(final, grad, gsum)
     return outs[0], outs[1], outs[2], outs[3], outs[4].reshape(HID)
 

time: 56.6 us -> 48.8 us (0.86)
  Pallas kernels: 55.8 us -> 48 us
    pallas_call x1, Pallas kernels: 54.2 us -> 47.3 us  [on_device(): pl.pallas_call(kernel, out_shape=(slab, slab, block), in_specs=[hbm] * 10...]
    pallas_call x1, Pallas kernels: 1.7 us -> 0.72 us  [on_device(): pl.pallas_call(hand_out, out_shape=(slab, slab, jax.ShapeDtypeStruct(conv...]
where the time goes in v3:
time: 48.8 us; the launch traced here: 48.7 us
  Pallas kernels  48 us (98%)
  between operations  0.64 us (1%)
    pallas_call x1, Pallas kernels, on_device(): pl.pallas_call(kernel, out_shape=(slab, slab, block), in_specs=[hbm] * 10...  47.3 us

profile of v3, /device:TPU:1, one launch (start us, length us, event | category | flops | bytes accessed | tf_op | source)
XLA Modules:
  0.0 48.7 jit_solution(5827823257078236758)
XLA Ops:
  0.6 47.3 %shard_map.137 = (f32[1,16,2048]{2,1,0:T(8,128)S(1)}, f32[1,16,2048]{2,1,0:T(8,128)S(1)}, f32[64,128]{1,0:T(8,128)S(1)}) custom-call(f32[1,16,2048]{2,1,0:T(8,128)} %film_hbm.1, f32[1,16,2048]{2,1,0:T(8,128)} %evap_hbm.1, s32[1,16,2048]{2,1,0:T(8,128)} %mask_hbm.1, s32[1,16,2048]{2,1,0:T(8,128)} %bitcast.3, s32[1,16,16]{2,1,0:T(8,128)} %scls_hbm.1, ...), custom_call_target="tpu_custom_call" | custom-call | tf_op jit(solution)/shard_map/pallas_call | solution.py:686
  47.9 0.7 %shard_map.138 = (f32[1,16,2048]{2,1,0:T(8,128)}, f32[1,16,2048]{2,1,0:T(8,128)}, f32[3,3,4,64]{3,2,1,0:T(4,128)}, f32[64,64]{1,0:T(8,128)}, f32[1,64]{1,0:T(1,128)}) custom-call(f32[1,16,2048]{2,1,0:T(8,128)S(1)} %get-tuple-element.13.final_in, f32[1,16,2048]{2,1,0:T(8,128)S(1)} %get-tuple-element.14.grad_in, f32[64,128]{1,0:T(8,128)S(1)} %get-tuple-element.15.gsum_in), custom_call_target="tpu_custom_call" | custom-call | tf_op jit(solution)/shard_map/pallas_call | solution.py:749

commit v4 on v3

--- a/solution.py
+++ b/solution.py
@@ -131,7 +131,6 @@
     sa_ref,
     u_ref,
     v_ref,
-    la_ref,
     srcf_ref,
     src_ref,
     back_ref,
@@ -166,6 +165,9 @@
         pltpu.make_async_copy(hbm, ref, in_sem.at[n])
         for n, (hbm, ref) in enumerate(
             (
+                (convw_hbm, convw_ref),
+                (mixw_hbm, mixw_ref),
+                (fluxw_hbm, fluxw_ref),
                 (cot_hbm, cot_ref),
                 (inv_hbm, inv_ref),
                 (scls_hbm, scls_ref),
@@ -173,16 +175,12 @@
                 (evap_hbm, evap_ref),
                 (mask_hbm, mask_ref),
                 (fcls_hbm, fcls_ref),
-                (convw_hbm, convw_ref),
-                (mixw_hbm, mixw_ref),
-                (fluxw_hbm, fluxw_ref),
             )
         )
     ]
-    for copy in inputs[:3]:
+    for copy in inputs[:6]:
         copy.start()
     side = film_ref.shape[2]
-    nblocks = side // WIDTH
     sp = lax.axis_index("sp")
     rep = lax.axis_index("rep")
     nsp = DYLO * DZ * DX
@@ -198,9 +196,6 @@
     def at(r, s):
         return {"rep": r, "sp": s}
 
-    up = mod(sp + nsp - 1, nsp)
-    down = mod(sp + 1, nsp)
-
     def group_peer(s):
         return at(rep, first + mod(member + s, GROUP))
 
@@ -221,12 +216,27 @@
         )
 
     barrier = pltpu.get_barrier_semaphore()
-    peers = [at(rep, up), at(rep, down)]
-    for s in range(1, 8):
-        peers += [group_peer(s), corner_peer(s), z_peer(s), y_peer(s)]
+    def signal(peer):
+        pl.semaphore_signal(barrier, inc=1, device_id=peer, device_id_type=MESH)
+
+    peers = [group_peer(s) for s in range(1, GROUP)]
+    peers += [corner_peer(s) for s in range(1, 8)]
+    peers += [z_peer(s) for s in range(1, 8)]
+    peers += [y_peer(s) for s in range(1, 8)]
+    has_up = sp > 0
+    has_down = sp < nsp - 1
     for peer in peers:
-        pl.semaphore_signal(barrier, inc=1, device_id=peer, device_id_type=MESH)
-    for copy in inputs[3:]:
+        signal(peer)
+
+    @pl.when(has_up)
+    def _():
+        signal(at(rep, sp - 1))
+
+    @pl.when(has_down)
+    def _():
+        signal(at(rep, sp + 1))
+
+    for copy in inputs[6:]:
         copy.start()
 
     def remote(src, dst, ssem, rsem, peer):
@@ -241,98 +251,6 @@
 
     for copy in inputs[:3]:
         copy.wait()
-    inv_hi, inv_lo = split2(inv_ref[...].reshape(NCLS * SPAN, SPAN))
-    for c in range(NCLS):
-        of = slice(c * SPAN, (c + 1) * SPAN)
-        t_hi, t_lo = split2(inv_ref[c].T)
-        invs_ref[0, 0, c] = t_hi
-        invs_ref[0, 1, c] = t_lo
-        invs_ref[1, 0, c] = inv_hi[of]
-        invs_ref[1, 1, c] = inv_lo[of]
-
-    nspan = side // SPAN
-    lines = jnp.concatenate(
-        [cot_ref[0, :, k * SPAN : (k + 1) * SPAN] for k in range(nspan)], axis=0
-    )
-    l_hi, l_lo = split2(lines)
-    right_hi = jnp.concatenate([inv_hi[c * SPAN : (c + 1) * SPAN] for c in range(NCLS)], axis=1)
-    right_lo = jnp.concatenate([inv_lo[c * SPAN : (c + 1) * SPAN] for c in range(NCLS)], axis=1)
-    products = nn(l_hi, right_hi) + nn(l_lo, right_hi) + nn(l_hi, right_lo)
-
-    def store_back(k, value):
-        back_ref[:, k * SPAN : (k + 1) * SPAN] = value.astype(BF)
-
-    span_select(products, scls_ref, store_back)
-    own_rows = pl.ds(pl.multiple_of(member * ROWS, ROWS), ROWS)
-    chunk = side // GROUP
-
-    def columns_of(n):
-        return pl.ds(pl.multiple_of(n * chunk, chunk), chunk)
-
-    def rows_of(n):
-        return pl.ds(pl.multiple_of(n * ROWS, ROWS), ROWS)
-
-    def span_out(which, field):
-        recv_ref[which, own_rows, :] = field[:, columns_of(member)]
-        for s in range(1, GROUP):
-            remote(
-                field.at[:, columns_of(mod(member + s, GROUP))],
-                recv_ref.at[which, own_rows],
-                ag_ssem.at[2 * which],
-                ag_rsem.at[2 * which],
-                group_peer(s),
-            ).start()
-
-    def span_solve(which, field, result):
-        others = GROUP - 1
-        remote(
-            field.at[:, pl.ds(0, others * chunk)],
-            recv_ref.at[which, pl.ds(0, others * ROWS)],
-            ag_ssem.at[2 * which],
-            ag_rsem.at[2 * which],
-            group_peer(1),
-        ).wait()
-        values = recv_ref[which]
-        line_cls = fcls_ref[0, :, columns_of(member)]
-        own_span = iota(line_cls.shape, 0) == div(sp, GROUP)
-        classes = jnp.sum(jnp.where(own_span, line_cls, 0), axis=0, keepdims=True)
-        solved = None
-        for c in range(NCLS):
-            product = nn(invs_ref[which, 0, c], values) + nn(invs_ref[which, 1, c], values)
-            solved = product if c == 0 else jnp.where(classes == c, product, solved)
-        mid_ref[which] = solved.astype(BF)
-        result[:, columns_of(member)] = mid_ref[which, own_rows, :]
-        for s in range(1, GROUP):
-            remote(
-                mid_ref.at[which, rows_of(mod(member + s, GROUP))],
-                result.at[:, columns_of(member)],
-                ag_ssem.at[2 * which + 1],
-                ag_rsem.at[2 * which + 1],
-                group_peer(s),
-            ).start()
-
-    def span_in(which, result):
-        others = GROUP - 1
-        remote(
-            mid_ref.at[which, pl.ds(0, others * ROWS)],
-            result.at[:, pl.ds(0, others * chunk)],
-            ag_ssem.at[2 * which + 1],
-            ag_rsem.at[2 * which + 1],
-            group_peer(1),
-        ).wait()
-
-    for copy in inputs[3:]:
-        copy.wait()
-
-    film = film_ref[0]
-    evap = evap_ref[0]
-    maskf = mask_ref[0].astype(F32)
-    for c, feature in enumerate((film, film * film, maskf, evap)):
-        feature = feature.astype(BF).astype(F32)
-        padf_ref[c, 1 : ROWS + 1, :] = feature
-        padf_ref[c, ROWS + 2 :, :] = jnp.zeros((6, side), F32)
-        halo_s[0, c : c + 1, :] = feature[0:1]
-        halo_s[1, c : c + 1, :] = feature[ROWS - 1 :]
 
     w36_ref[...] = jnp.zeros_like(w36_ref)
     for a in range(3):
@@ -371,8 +289,140 @@
     fw_col = jnp.sum(
         jnp.where(eye, jnp.broadcast_to(fw.astype(F32), (HID, HID)), 0.0), axis=1, keepdims=True
     )
-    fwc_ref[...] = jnp.concatenate([jnp.broadcast_to(fw_col, (HID, WIDTH))] * 4, axis=0)
-
+    fwc_ref[...] = jnp.concatenate([jnp.broadcast_to(fw_col, (HID, 2 * WIDTH))] * 4, axis=0)
+
+    for copy in inputs[3:6]:
+        copy.wait()
+    inv_hi, inv_lo = split2(inv_ref[...].reshape(NCLS * SPAN, SPAN))
+    for c in range(NCLS):
+        of = slice(c * SPAN, (c + 1) * SPAN)
+        t_hi, t_lo = split2(inv_ref[c].T)
+        invs_ref[0, 0, c] = t_hi
+        invs_ref[0, 1, c] = t_lo
+        invs_ref[1, 0, c] = inv_hi[of]
+        invs_ref[1, 1, c] = inv_lo[of]
+
+    nspan = side // SPAN
+    lines = jnp.concatenate(
+        [cot_ref[0, :, k * SPAN : (k + 1) * SPAN] for k in range(nspan)], axis=0
+    )
+    l_hi, l_lo = split2(lines)
+    right_hi = jnp.concatenate([inv_hi[c * SPAN : (c + 1) * SPAN] for c in range(NCLS)], axis=1)
+    right_lo = jnp.concatenate([inv_lo[c * SPAN : (c + 1) * SPAN] for c in range(NCLS)], axis=1)
+    products = nn(l_hi, right_hi) + nn(l_lo, right_hi) + nn(l_hi, right_lo)
+
+    def store_back(k, value):
+        back_ref[:, k * SPAN : (k + 1) * SPAN] = value.astype(BF)
+
+    span_select(products, scls_ref, store_back)
+    own_rows = pl.ds(pl.multiple_of(member * ROWS, ROWS), ROWS)
+    chunk = side // GROUP
+
+    def columns_of(n):
+        return pl.ds(pl.multiple_of(n * chunk, chunk), chunk)
+
+    def rows_of(n):
+        return pl.ds(pl.multiple_of(n * ROWS, ROWS), ROWS)
+
+    def span_out(which, field):
+        recv_ref[which, own_rows, :] = field[:, columns_of(member)]
+        for s in range(1, GROUP):
+            remote(
+                field.at[:, columns_of(mod(member + s, GROUP))],
+                recv_ref.at[which, own_rows],
+                ag_ssem.at[2 * which],
+                ag_rsem.at[2 * which],
+                group_peer(s),
+            ).start()
+
+    def span_solve(which, field, result):
+        others = GROUP - 1
+        remote(
+            field.at[:, pl.ds(0, others * chunk)],
+            recv_ref.at[which, pl.ds(0, others * ROWS)],
+            ag_ssem.at[2 * which],
+            ag_rsem.at[2 * which],
+            group_peer(1),
+        ).wait()
+        values = recv_ref[which]
+        line_cls = fcls_ref[0, :, columns_of(member)]
+        own_span = iota(line_cls.shape, 0) == div(sp, GROUP)
+        classes = jnp.sum(jnp.where(own_span, line_cls, 0), axis=0, keepdims=True)
+        solved = None
+        for c in range(NCLS):
+            product = nn(invs_ref[which, 0, c], values) + nn(invs_ref[which, 1, c], values)
+            solved = product if c == 0 else jnp.where(classes == c, product, solved)
+        mid_ref[which] = solved.astype(BF)
+        result[:, columns_of(member)] = mid_ref[which, own_rows, :]
+        for s in range(1, GROUP):
+            remote(
+                mid_ref.at[which, rows_of(mod(member + s, GROUP))],
+                result.at[:, columns_of(member)],
+                ag_ssem.at[2 * which + 1],
+                ag_rsem.at[2 * which + 1],
+                group_peer(s),
+            ).start()
+
+    def span_in(which, result):
+        others = GROUP - 1
+        remote(
+            mid_ref.at[which, pl.ds(0, others * ROWS)],
+            result.at[:, pl.ds(0, others * chunk)],
+            ag_ssem.at[2 * which + 1],
+            ag_rsem.at[2 * which + 1],
+            group_peer(1),
+        ).wait()
+
+    for copy in inputs[6:]:
+        copy.wait()
+
+    film = film_ref[0]
+    evap = evap_ref[0]
+    maskf = mask_ref[0].astype(F32)
+    features = [f.astype(BF).astype(F32) for f in (film, film * film, maskf, evap)]
+    for c, feature in enumerate(features):
+        padf_ref[c, 0:1, :] = jnp.zeros((1, side), F32)
+        padf_ref[c, 1 : ROWS + 1, :] = feature
+        padf_ref[c, ROWS + 1 :, :] = jnp.zeros((7, side), F32)
+    halo_s[0] = jnp.concatenate([f[0:1] for f in features], axis=0).astype(BF)
+    halo_s[1] = jnp.concatenate([f[ROWS - 1 :] for f in features], axis=0).astype(BF)
+
+    def to_neighbours(n, sent, landed):
+        upward = remote(
+            sent.at[0], landed.at[1], nb_ssem.at[n, 0], nb_rsem.at[n, 0], at(rep, sp - 1)
+        )
+        downward = remote(
+            sent.at[1], landed.at[0], nb_ssem.at[n, 1], nb_rsem.at[n, 1], at(rep, sp + 1)
+        )
+        return upward, downward
+
+    def exchange_start(n, sent, landed):
+        upward, downward = to_neighbours(n, sent, landed)
+
+        @pl.when(has_up)
+        def _():
+            upward.start()
+
+        @pl.when(has_down)
+        def _():
+            downward.start()
+
+    def exchange_wait(n, sent, landed, use):
+        upward, downward = to_neighbours(n, sent, landed)
+
+        @pl.when(has_up)
+        def _():
+            upward.wait_send()
+            downward.wait_recv()
+            use(landed[0].astype(F32), 0)
+
+        @pl.when(has_down)
+        def _():
+            downward.wait_send()
+            upward.wait_recv()
+            use(landed[1].astype(F32), ROWS + 1)
+
+    wide = 2 * WIDTH
     lane = iota((24, side), 1)
 
     def build_pieces(g):
@@ -390,37 +440,39 @@
 
     def forward(g):
         def body(i, carry):
-            def cols_at(n):
-                start = pl.multiple_of(i * (2 * WIDTH) + n * WIDTH, WIDTH)
-                return pl.ds(start, WIDTH)
-
-            def first_layer(n):
-                cols = cols_at(n)
-                t1 = jnp.tanh(nn(wb_ref[g, :, : PIECES * 16], x_ref[g, :, cols]))
+            cols = pl.ds(pl.multiple_of(i * wide, wide), wide)
+            factors = {}
+
+            def rows_at(q):
+                return slice(q * WIDTH, (q + 1) * WIDTH)
+
+            def conv(q):
+                return nn(wb_ref[g, rows_at(q), : PIECES * 16], x_ref[g, :, cols])
+
+            def first_act(q, total):
+                of = rows_at(q)
+                t1 = jnp.tanh(total)
                 a1 = t1.astype(BF)
-                a1_ref[g, :, cols] = a1
-                la_ref[n] = a1
-                d1_ref[n] = 1.0 - t1 * t1
-
-            factors = {}
-
-            def second_layer(n, q):
-                of = slice(q * WIDTH, (q + 1) * WIDTH)
-                cols = cols_at(n)
-                t2 = jnp.tanh(nn(bdf_ref[...], la_ref[n, of, :]))
-                sa_ref[g, of, cols] = t2.astype(BF)
+                a1_ref[g, of, cols] = a1
+                d1_ref[of, :] = 1.0 - t1 * t1
+                return nn(bdf_ref[...], a1)
+
+            def second_act(q, total):
+                of = rows_at(q)
+                t2 = jnp.tanh(total)
+                active = t2.astype(BF)
+                sa_ref[g, of, cols] = active
                 u = (fwc_ref[...] * (1.0 - t2 * t2)).astype(BF)
                 u_ref[g, of, cols] = u
-                factors[n, q] = (u, t2.astype(BF))
-
-            def combine(n, q):
-                of = slice(q * WIDTH, (q + 1) * WIDTH)
-                v = d1_ref[n, of, :] * nn(bdb_ref[...], factors[n, q][0])
-                v_ref[g, of, cols_at(n)] = v.astype(BF)
-
-            def sources(n):
-                cols = cols_at(n)
-                sa = jnp.concatenate([factors[n, 0][1], factors[n, 1][1]], axis=0)
+                factors[q] = (u, active)
+                return nn(bdb_ref[...], u)
+
+            def combine(q, total):
+                of = rows_at(q)
+                v_ref[g, of, cols] = (d1_ref[of, :] * total).astype(BF)
+
+            def sources():
+                sa = jnp.concatenate([factors[0][1], factors[1][1]], axis=0)
                 flux = nn(fwb_ref[...], sa)[:HALF]
                 drain = mask_ref[0, :, cols].astype(F32) * evap_ref[0, :, cols]
                 rest = film_ref[0, :, cols] - TIME_STEP * drain
@@ -432,39 +484,35 @@
                     srcf_ref[0:quarter, cols] = source[:quarter]
                     srcf_ref[quarter + HALF :, cols] = source[quarter:]
 
-            first_layer(0)
-            second_layer(0, 0)
-            first_layer(1)
-            second_layer(0, 1)
-            combine(0, 0)
-            second_layer(1, 0)
-            combine(0, 1)
-            sources(0)
-            second_layer(1, 1)
-            combine(1, 0)
-            combine(1, 1)
-            sources(1)
+            one0 = conv(0)
+            one1 = conv(1)
+            two0 = first_act(0, one0)
+            two1 = first_act(1, one1)
+            three0 = second_act(0, two0)
+            three1 = second_act(1, two1)
+            combine(0, three0)
+            sources()
+            combine(1, three1)
             return carry
 
         return body
 
-    pairs = nblocks // 2
+    pairs = side // wide
     build_pieces(0)
     lax.fori_loop(0, 1, forward(0), 0)
 
-    pl.semaphore_wait(barrier, len(peers))
-    remote(halo_s.at[0], halo_r.at[1], nb_ssem.at[0], nb_rsem.at[0], at(rep, up)).start()
-    remote(halo_s.at[1], halo_r.at[0], nb_ssem.at[0], nb_rsem.at[0], at(rep, down)).start()
+    neighbours = jnp.where(has_up, 1, 0) + jnp.where(has_down, 1, 0)
+    pl.semaphore_wait(barrier, len(peers) + neighbours)
+    exchange_start(0, halo_s, halo_r)
     span_out(0, back_ref)
 
     lax.fori_loop(1, pairs, forward(0), 0)
 
-    remote(halo_s, halo_r, nb_ssem.at[0], nb_rsem.at[0], at(rep, up)).wait()
-    for c in range(CIN):
-        padf_ref[c, 0:1, :] = jnp.where(sp > 0, halo_r[0, c : c + 1, :], 0.0)
-        padf_ref[c, ROWS + 1 : ROWS + 2, :] = jnp.where(
-            sp < nsp - 1, halo_r[1, c : c + 1, :], 0.0
-        )
+    def set_rim(values, row):
+        for c in range(CIN):
+            padf_ref[c, row : row + 1, :] = values[c : c + 1]
+
+    exchange_wait(0, halo_s, halo_r, set_rim)
     build_pieces(1)
     span_solve(0, back_ref, sg_ref)
     lax.fori_loop(0, pairs, forward(1), 0)
@@ -476,27 +524,37 @@
     macc_ref[...] = jnp.zeros_like(macc_ref)
     facc_ref[...] = jnp.zeros_like(facc_ref)
 
+    def add_products(g, q, mixing, taps):
+        macc_ref[q] += mixing
+        cacc_ref[g, q * WIDTH : (q + 1) * WIDTH, :] += taps
+
     def backward(i, carry):
-        cols = pl.ds(pl.multiple_of(i * WIDTH, WIDTH), WIDTH)
-        mixing = macc_ref[...]
+        cols = pl.ds(pl.multiple_of(i * wide, wide), wide)
         flux_cots = TIME_STEP * sg_ref[:, cols].astype(F32)
+        products = []
         for g in range(2):
-            firsts = []
-            for r in range(HALF):
-                of = slice(r * HID, (r + 1) * HID)
-                at_row = row_of(g, r)
-                row = jnp.broadcast_to(flux_cots[at_row : at_row + 1], (HID, WIDTH)).astype(BF)
-                mixing = mixing + nt(a1_ref[g, of, cols], u_ref[g, of, cols] * row)
-                firsts.append(v_ref[g, of, cols] * row)
-            pre_first = jnp.concatenate(firsts, axis=0)
-            v_ref[g, :, cols] = pre_first
+            for q in range(2):
+                of = slice(q * WIDTH, (q + 1) * WIDTH)
+                rows = jnp.concatenate(
+                    [
+                        jnp.broadcast_to(flux_cots[n : n + 1], (HID, wide)).astype(BF)
+                        for n in [row_of(g, 4 * q + r) for r in range(4)]
+                    ],
+                    axis=0,
+                )
+                pre_first = v_ref[g, of, cols] * rows
+                v_ref[g, of, cols] = pre_first
+                mixing = nt(a1_ref[g, of, cols], u_ref[g, of, cols] * rows)
+                taps = nt(pre_first, x_ref[g, :, cols])
+                products.append((g, q, mixing, taps))
+                if len(products) > 1:
+                    add_products(*products[-2])
             cots = group_rows(flux_cots, g).astype(BF)
             facc_ref[...] += nt(cots, sa_ref[g, :, cols])
-            cacc_ref[g] += nt(pre_first, x_ref[g, :, cols])
-        macc_ref[...] = mixing
+        add_products(*products[-1])
         return carry
 
-    lax.fori_loop(0, nblocks, backward, 0)
+    lax.fori_loop(0, side // wide, backward, 0)
 
     rolled = {}
     for g in range(2):
@@ -528,7 +586,12 @@
     flux_row = jnp.sum(flux_rows, axis=0, keepdims=True)
     right = right + jnp.where(iota((HID, 2 * HID), 0) == 9 * CIN, flux_row, 0.0)
     g_ref[...] = right
-    g_ref[:, 0:HID] = macc_ref[...]
+    blocks = []
+    for r in range(4):
+        of, at_span = slice(r * HID, (r + 1) * HID), slice((r // 2) * SPAN, (r // 2 + 1) * SPAN)
+        blocks.append(macc_ref[0, of, at_span] + macc_ref[1, of, at_span])
+    mixing = blocks[0] + blocks[2] + pltpu.roll(blocks[1] + blocks[3], HID, axis=1)
+    g_ref[:, 0:HID] = mixing[:, 0:HID]
 
     own_block = pl.ds(pl.multiple_of(j_at * 8, 8), 8)
     p1_ref[j_at] = g_ref[own_block, :]
@@ -550,12 +613,12 @@
     span_solve(1, src_ref, across_ref)
 
     def features_back(i, carry):
-        cols = pl.ds(pl.multiple_of(i * WIDTH, WIDTH), WIDTH)
+        cols = pl.ds(pl.multiple_of(i * wide, wide), wide)
         for h in range(2):
             tt_ref[h, :, cols] = nn(wct_ref[h], v_ref[h, :, cols])
         return carry
 
-    lax.fori_loop(0, nblocks, features_back, 0)
+    lax.fori_loop(0, side // wide, features_back, 0)
 
     def finish(stage, slots, send_peer):
         remote(
@@ -601,8 +664,7 @@
         tot_ref[c, 4:20, :] += parts[0]
         rim_s[0, c : c + 1, :] = parts[1][0:1]
         rim_s[1, c : c + 1, :] = parts[1][13:14]
-    remote(rim_s.at[0], rim_r.at[1], nb_ssem.at[1], nb_rsem.at[1], at(rep, up)).start()
-    remote(rim_s.at[1], rim_r.at[0], nb_ssem.at[1], nb_rsem.at[1], at(rep, down)).start()
+    exchange_start(1, rim_s, rim_r)
 
     span_in(1, across_ref)
     pieces = [across_ref[:, k * SPAN : (k + 1) * SPAN] for k in range(nspan)]
@@ -623,10 +685,12 @@
     p3_ref[y_at] = q2_ref[...]
     begin(2, p3_ref, y_at, q2_ref, y_peer)
 
-    remote(rim_s, rim_r, nb_ssem.at[1], nb_rsem.at[1], at(rep, up)).wait()
-    for c in range(2):
-        tot_ref[c, 1:2, :] += jnp.where(sp > 0, rim_r[0, c : c + 1, :], 0.0)
-        tot_ref[c, ROWS : ROWS + 1, :] += jnp.where(sp < nsp - 1, rim_r[1, c : c + 1, :], 0.0)
+    def add_rim(values, row):
+        for c in range(2):
+            at_row = 1 if row == 0 else ROWS
+            tot_ref[c, at_row : at_row + 1, :] += values[c : c + 1]
+
+    exchange_wait(1, rim_s, rim_r, add_rim)
     cot0 = tot_ref[0, 1 : ROWS + 1, :].astype(BF).astype(F32)
     cot1 = tot_ref[1, 1 : ROWS + 1, :].astype(BF).astype(F32)
     grad_ref[0] = sg_ref[...].astype(F32) + cot0 + 2.0 * film_ref[0] * cot1
@@ -696,8 +760,8 @@
             pltpu.VMEM((2, 2, NCLS, SPAN, SPAN), BF),
             pltpu.VMEM((2, SPAN, chunk), BF),
             pltpu.VMEM((2, SPAN, chunk), BF),
-            pltpu.VMEM((2, CIN, side), F32),
-            pltpu.VMEM((2, CIN, side), F32),
+            pltpu.VMEM((2, CIN, side), BF),
+            pltpu.VMEM((2, CIN, side), BF),
             pltpu.VMEM((CIN, 24, side), F32),
             pltpu.VMEM((2, PIECES * 16, side), BF),
             pltpu.VMEM((2, tall, WIDTH), BF),
@@ -705,20 +769,19 @@
             pltpu.VMEM((WIDTH, WIDTH), BF),
             pltpu.VMEM((WIDTH, WIDTH), BF),
             pltpu.VMEM((16, tall), BF),
-            pltpu.VMEM((WIDTH, WIDTH), F32),
+            pltpu.VMEM((WIDTH, 2 * WIDTH), F32),
             pltpu.VMEM((2, tall, side), BF),
-            pltpu.VMEM((2, tall, WIDTH), F32),
+            pltpu.VMEM((tall, 2 * WIDTH), F32),
             pltpu.VMEM((2, tall, side), BF),
             pltpu.VMEM((2, tall, side), BF),
             pltpu.VMEM((2, tall, side), BF),
-            pltpu.VMEM((2, tall, WIDTH), BF),
             pltpu.VMEM((rows, side), F32),
             pltpu.VMEM((rows, side), BF),
             pltpu.VMEM((rows, side), BF),
             pltpu.VMEM((rows, side), BF),
             pltpu.VMEM((rows, side), BF),
             pltpu.VMEM((2, tall, PIECES * 16), F32),
-            pltpu.VMEM((HID, HID), F32),
+            pltpu.VMEM((2, WIDTH, WIDTH), F32),
             pltpu.VMEM((HALF, tall), F32),
             pltpu.VMEM((2, 96, side), F32),
             pltpu.VMEM((2, 24, side), F32),
@@ -737,8 +800,8 @@
             pltpu.SemaphoreType.DMA((3,)),
             pltpu.SemaphoreType.DMA((4,)),
             pltpu.SemaphoreType.DMA((4,)),
-            pltpu.SemaphoreType.DMA((2,)),
-            pltpu.SemaphoreType.DMA((2,)),
+            pltpu.SemaphoreType.DMA((2, 2)),
+            pltpu.SemaphoreType.DMA((2, 2)),
             pltpu.SemaphoreType.DMA((4,)),
             pltpu.SemaphoreType.DMA((4,)),
         ],

time: 48.8 us -> 47.5 us (0.973)
  Pallas kernels: 48 us -> 46.7 us
    pallas_call x1, Pallas kernels: 47.3 us -> 46 us  [on_device(): pl.pallas_call(kernel, out_shape=(slab, slab, block), in_specs=[hbm] * 10...]
where the time goes in v4:
time: 47.5 us; the launch traced here: 47.4 us
  Pallas kernels  46.7 us (98%)
  between operations  0.64 us (1%)
    pallas_call x1, Pallas kernels, on_device(): pl.pallas_call(kernel, out_shape=(slab, slab, block), in_specs=[hbm] * 10...  46 us

profile of v4, /device:TPU:1, one launch (start us, length us, event | category | flops | bytes accessed | tf_op | source)
XLA Modules:
  0.0 47.4 jit_solution(715141700428205796)
XLA Ops:
  0.6 46.0 %shard_map.137 = (f32[1,16,2048]{2,1,0:T(8,128)S(1)}, f32[1,16,2048]{2,1,0:T(8,128)S(1)}, f32[64,128]{1,0:T(8,128)S(1)}) custom-call(f32[1,16,2048]{2,1,0:T(8,128)} %film_hbm.1, f32[1,16,2048]{2,1,0:T(8,128)} %evap_hbm.1, s32[1,16,2048]{2,1,0:T(8,128)} %mask_hbm.1, s32[1,16,2048]{2,1,0:T(8,128)} %bitcast.3, s32[1,16,16]{2,1,0:T(8,128)} %scls_hbm.1, ...), custom_call_target="tpu_custom_call" | custom-call | tf_op jit(solution)/shard_map/pallas_call | solution.py:750
  46.6 0.7 %shard_map.138 = (f32[1,16,2048]{2,1,0:T(8,128)}, f32[1,16,2048]{2,1,0:T(8,128)}, f32[3,3,4,64]{3,2,1,0:T(4,128)}, f32[64,64]{1,0:T(8,128)}, f32[1,64]{1,0:T(1,128)}) custom-call(f32[1,16,2048]{2,1,0:T(8,128)S(1)} %get-tuple-element.13.final_in, f32[1,16,2048]{2,1,0:T(8,128)S(1)} %get-tuple-element.14.grad_in, f32[64,128]{1,0:T(8,128)S(1)} %get-tuple-element.15.gsum_in), custom_call_target="tpu_custom_call" | custom-call | tf_op jit(solution)/shard_map/pallas_call | solution.py:812

commit v5 on v4

--- a/solution.py
+++ b/solution.py
@@ -12,7 +12,6 @@
 MESH = pl.DeviceIdType.MESH
 SPAN = 128
 ROWS = 16
-HALF = 8
 HID = 64
 CIN = 4
 PIECES = 12
@@ -51,21 +50,29 @@
     return lax.div(a, jnp.int32(n))
 
 
-def shift_of(group, r):
-    return r if group == 0 or r < HALF // 2 else r + HALF // 2
-
-
-def row_of(group, r):
+EDGE = 2
+ORDER = list(range(EDGE, ROWS - EDGE)) + [0, 1, ROWS - 2, ROWS - 1]
+SHIFTS = list(range(ROWS - 2 * EDGE)) + [0, 1, 8, 9]
+CHUNKS = ((0, 1, 2), (3,))
+COUNTS = (ROWS - 2 * EDGE, 2 * EDGE)
+
+
+def group_of(m):
+    return 0 if m in CHUNKS[0] else 1
+
+
+def chunk_rows(m):
+    return slice(m * WIDTH, (m + 1) * WIDTH)
+
+
+def group_part(g):
+    return slice(CHUNKS[g][0] * WIDTH, (CHUNKS[g][-1] + 1) * WIDTH)
+
+
+def group_rows(values, group):
     if group == 0:
-        return r + HALF // 2
-    return r if r < HALF // 2 else r + HALF
-
-
-def group_rows(values, group):
-    quarter = HALF // 2
-    if group == 0:
-        return values[quarter : quarter + HALF]
-    return jnp.concatenate([values[:quarter], values[quarter + HALF :]], axis=0)
+        return values[EDGE : ROWS - EDGE]
+    return jnp.concatenate([values[:EDGE], values[ROWS - EDGE :]], axis=0)
 
 
 def iota(shape, dim):
@@ -160,6 +167,7 @@
     nb_rsem,
     ar_ssem,
     ar_rsem,
+    far_sem,
 ):
     inputs = [
         pltpu.make_async_copy(hbm, ref, in_sem.at[n])
@@ -221,8 +229,8 @@
 
     peers = [group_peer(s) for s in range(1, GROUP)]
     peers += [corner_peer(s) for s in range(1, 8)]
-    peers += [z_peer(s) for s in range(1, 8)]
-    peers += [y_peer(s) for s in range(1, 8)]
+    beside = [z_peer(1), z_peer(7), y_peer(1), y_peer(7)]
+    peers += beside
     has_up = sp > 0
     has_down = sp < nsp - 1
     for peer in peers:
@@ -265,13 +273,11 @@
     wanted = (tap_row * 3 + piece % 3) * CIN + piece // 3
     pick = (k_at == wanted) & (tap_row < 3) & (piece < PIECES)
     band0 = nn(w_t, onehot(pick))
-    for g in range(2):
-        shifts = [shift_of(g, r) for r in range(HALF)]
-        band = jnp.concatenate(
-            [band0 if n == 0 else pltpu.roll(band0, n, axis=1) for n in shifts], axis=0
-        )
-        wb_ref[g] = band.astype(BF)
-        wct_ref[g] = band[:, :SPAN].T[:96].astype(BF)
+    rolls = [band0 if n == 0 else pltpu.roll(band0, n, axis=1) for n in range(max(SHIFTS) + 1)]
+    for m in range(4):
+        band = jnp.concatenate([rolls[n] for n in SHIFTS[4 * m : 4 * m + 4]], axis=0)
+        wb_ref[chunk_rows(m), :] = band.astype(BF)
+        wct_ref[:, chunk_rows(m)] = band[:, :SPAN].T[:96].astype(BF)
     mix = mixw_ref[...]
     tile4 = onehot(iota((HID, WIDTH), 1) % HID == iota((HID, WIDTH), 0))
     wide = nn(mix, tile4)
@@ -281,9 +287,9 @@
     bdb_ref[...] = diag.astype(BF)
     bdf_ref[...] = diag.T.astype(BF)
     fw = fluxw_ref[...]
-    tile8 = onehot(iota((HID, HALF * HID), 1) % HID == iota((HID, HALF * HID), 0))
+    tile8 = onehot(mod(iota((HID, 3 * WIDTH), 1), HID) == iota((HID, 3 * WIDTH), 0))
     fw_wide = nn(jnp.broadcast_to(fw, (16, HID)), tile8)
-    own = iota((16, HALF * HID), 1) // HID == iota((16, HALF * HID), 0)
+    own = div(iota((16, 3 * WIDTH), 1), HID) == iota((16, 3 * WIDTH), 0)
     fwb_ref[...] = jnp.where(own, fw_wide, 0.0).astype(BF)
     eye = iota((HID, HID), 0) == iota((HID, HID), 1)
     fw_col = jnp.sum(
@@ -433,80 +439,100 @@
             for b, values in enumerate((left, middle, right)):
                 s = (c * 3 + b) * 16
                 if g == 0:
-                    piece = values[4:20]
+                    piece = values[EDGE : EDGE + 16]
                 else:
-                    piece = jnp.concatenate([values[0:8], values[12:20]], axis=0)
+                    piece = jnp.concatenate([values[0:8], values[14:22]], axis=0)
                 x_ref[g, s : s + 16, :] = piece.astype(BF)
 
-    def forward(g):
+    def forward(g, blocks):
+        units = [(m, n) for n in range(blocks) for m in CHUNKS[g]]
+
         def body(i, carry):
-            cols = pl.ds(pl.multiple_of(i * wide, wide), wide)
             factors = {}
 
-            def rows_at(q):
-                return slice(q * WIDTH, (q + 1) * WIDTH)
-
-            def conv(q):
-                return nn(wb_ref[g, rows_at(q), : PIECES * 16], x_ref[g, :, cols])
-
-            def first_act(q, total):
-                of = rows_at(q)
+            def cols_at(n):
+                return pl.ds(pl.multiple_of((i * blocks + n) * wide, wide), wide)
+
+            def conv(m, n):
+                return nn(wb_ref[chunk_rows(m), : PIECES * 16], x_ref[g, :, cols_at(n)])
+
+            def first_act(m, n, total):
                 t1 = jnp.tanh(total)
                 a1 = t1.astype(BF)
-                a1_ref[g, of, cols] = a1
-                d1_ref[of, :] = 1.0 - t1 * t1
+                a1_ref[chunk_rows(m), cols_at(n)] = a1
+                d1_ref[units.index((m, n))] = 1.0 - t1 * t1
                 return nn(bdf_ref[...], a1)
 
-            def second_act(q, total):
-                of = rows_at(q)
+            def second_act(m, n, total):
                 t2 = jnp.tanh(total)
                 active = t2.astype(BF)
-                sa_ref[g, of, cols] = active
+                sa_ref[chunk_rows(m), cols_at(n)] = active
                 u = (fwc_ref[...] * (1.0 - t2 * t2)).astype(BF)
-                u_ref[g, of, cols] = u
-                factors[q] = (u, active)
+                u_ref[chunk_rows(m), cols_at(n)] = u
+                factors[m, n] = active
                 return nn(bdb_ref[...], u)
 
-            def combine(q, total):
-                of = rows_at(q)
-                v_ref[g, of, cols] = (d1_ref[of, :] * total).astype(BF)
-
-            def sources():
-                sa = jnp.concatenate([factors[0][1], factors[1][1]], axis=0)
-                flux = nn(fwb_ref[...], sa)[:HALF]
+            def combine(m, n, total):
+                v = d1_ref[units.index((m, n))] * total
+                v_ref[chunk_rows(m), cols_at(n)] = v.astype(BF)
+
+            def sources(n):
+                cols = cols_at(n)
+                sa = jnp.concatenate([factors[m, n] for m in CHUNKS[g]], axis=0)
+                flux = nn(fwb_ref[:, : sa.shape[0]], sa)[: COUNTS[g]]
                 drain = mask_ref[0, :, cols].astype(F32) * evap_ref[0, :, cols]
                 rest = film_ref[0, :, cols] - TIME_STEP * drain
                 source = group_rows(rest, g) + TIME_STEP * flux
-                quarter = HALF // 2
                 if g == 0:
-                    srcf_ref[quarter : quarter + HALF, cols] = source
+                    srcf_ref[EDGE : ROWS - EDGE, cols] = source
                 else:
-                    srcf_ref[0:quarter, cols] = source[:quarter]
-                    srcf_ref[quarter + HALF :, cols] = source[quarter:]
-
-            one0 = conv(0)
-            one1 = conv(1)
-            two0 = first_act(0, one0)
-            two1 = first_act(1, one1)
-            three0 = second_act(0, two0)
-            three1 = second_act(1, two1)
-            combine(0, three0)
-            sources()
-            combine(1, three1)
+                    srcf_ref[0:EDGE, cols] = source[:EDGE]
+                    srcf_ref[ROWS - EDGE :, cols] = source[EDGE:]
+
+            one = [conv(*unit) for unit in units[:2]]
+            two, three = [], []
+            for k, unit in enumerate(units):
+                two.append(first_act(*unit, one[k]))
+                if k + 2 < len(units):
+                    one.append(conv(*units[k + 2]))
+                if k >= 1:
+                    three.append(second_act(*units[k - 1], two[k - 1]))
+                if k >= 2:
+                    combine(*units[k - 2], three[k - 2])
+            three.append(second_act(*units[-1], two[-1]))
+            for k in range(max(0, len(units) - 2), len(units) - 1):
+                combine(*units[k], three[k])
+            for n in range(blocks):
+                sources(n)
+            combine(*units[-1], three[-1])
             return carry
 
         return body
 
     pairs = side // wide
     build_pieces(0)
-    lax.fori_loop(0, 1, forward(0), 0)
+    lax.fori_loop(0, 1, forward(0, 1), 0)
 
     neighbours = jnp.where(has_up, 1, 0) + jnp.where(has_down, 1, 0)
     pl.semaphore_wait(barrier, len(peers) + neighbours)
     exchange_start(0, halo_s, halo_r)
+
+    def tell(n):
+        for peer in beside:
+            pl.semaphore_signal(far_sem.at[n], inc=1, device_id=peer, device_id_type=MESH)
+
+    def hear(n):
+        pl.semaphore_wait(far_sem.at[n], len(beside))
+
+    tell(0)
     span_out(0, back_ref)
 
-    lax.fori_loop(1, pairs, forward(0), 0)
+    lax.fori_loop(1, pairs, forward(0, 1), 0)
+
+    span_solve(0, back_ref, sg_ref)
+
+    hear(0)
+    tell(1)
 
     def set_rim(values, row):
         for c in range(CIN):
@@ -514,8 +540,9 @@
 
     exchange_wait(0, halo_s, halo_r, set_rim)
     build_pieces(1)
-    span_solve(0, back_ref, sg_ref)
-    lax.fori_loop(0, pairs, forward(1), 0)
+    lax.fori_loop(0, pairs // 2, forward(1, 2), 0)
+    hear(1)
+    tell(2)
     src_ref[...] = srcf_ref[...].astype(BF)
     span_out(1, src_ref)
     span_in(0, sg_ref)
@@ -524,44 +551,42 @@
     macc_ref[...] = jnp.zeros_like(macc_ref)
     facc_ref[...] = jnp.zeros_like(facc_ref)
 
-    def add_products(g, q, mixing, taps):
-        macc_ref[q] += mixing
-        cacc_ref[g, q * WIDTH : (q + 1) * WIDTH, :] += taps
+    def add_products(m, mixing, taps):
+        macc_ref[m % 2] += mixing
+        cacc_ref[chunk_rows(m), :] += taps
 
     def backward(i, carry):
         cols = pl.ds(pl.multiple_of(i * wide, wide), wide)
         flux_cots = TIME_STEP * sg_ref[:, cols].astype(F32)
         products = []
-        for g in range(2):
-            for q in range(2):
-                of = slice(q * WIDTH, (q + 1) * WIDTH)
-                rows = jnp.concatenate(
-                    [
-                        jnp.broadcast_to(flux_cots[n : n + 1], (HID, wide)).astype(BF)
-                        for n in [row_of(g, 4 * q + r) for r in range(4)]
-                    ],
-                    axis=0,
-                )
-                pre_first = v_ref[g, of, cols] * rows
-                v_ref[g, of, cols] = pre_first
-                mixing = nt(a1_ref[g, of, cols], u_ref[g, of, cols] * rows)
-                taps = nt(pre_first, x_ref[g, :, cols])
-                products.append((g, q, mixing, taps))
-                if len(products) > 1:
-                    add_products(*products[-2])
-            cots = group_rows(flux_cots, g).astype(BF)
-            facc_ref[...] += nt(cots, sa_ref[g, :, cols])
+        for m in range(4):
+            of = chunk_rows(m)
+            rows = jnp.concatenate(
+                [
+                    jnp.broadcast_to(flux_cots[n : n + 1], (HID, wide)).astype(BF)
+                    for n in ORDER[4 * m : 4 * m + 4]
+                ],
+                axis=0,
+            )
+            pre_first = v_ref[of, cols] * rows
+            v_ref[of, cols] = pre_first
+            mixing = nt(a1_ref[of, cols], u_ref[of, cols] * rows)
+            taps = nt(pre_first, x_ref[group_of(m), :, cols])
+            products.append((m, mixing, taps))
+            if m > 0:
+                add_products(*products[m - 1])
+            if m == 1:
+                cots = jnp.concatenate([group_rows(flux_cots, g) for g in range(2)], axis=0)
+                facc_ref[...] += nt(cots.astype(BF), sa_ref[:, cols])
         add_products(*products[-1])
         return carry
 
     lax.fori_loop(0, side // wide, backward, 0)
 
     rolled = {}
-    for g in range(2):
-        for r in range(HALF):
-            n = shift_of(g, r)
-            term = cacc_ref[g, r * HID : (r + 1) * HID]
-            rolled[n] = term if n not in rolled else rolled[n] + term
+    for r, n in enumerate(SHIFTS):
+        term = cacc_ref[r * HID : (r + 1) * HID]
+        rolled[n] = term if n not in rolled else rolled[n] + term
     taps = jnp.zeros((HID, WIDTH), F32)
     spare = jnp.zeros((HID, WIDTH - PIECES * 16), F32)
     for n, term in rolled.items():
@@ -577,10 +602,10 @@
     right = jnp.zeros((HID, 2 * HID), F32)
     for t in split3(taps):
         right = right + nt(pick, jnp.concatenate([low, t], axis=0))
-    tall = HALF * HID
+    tall = ROWS * HID
     fold = onehot(mod(iota((tall, 2 * HID), 0), HID) + HID == iota((tall, 2 * HID), 1))
-    mine = div(iota((HALF, tall), 1), HID) == iota((HALF, tall), 0)
-    flux_rows = jnp.zeros((HALF, 2 * HID), F32)
+    mine = div(iota((ROWS, tall), 1), HID) == iota((ROWS, tall), 0)
+    flux_rows = jnp.zeros((ROWS, 2 * HID), F32)
     for f in split3(jnp.where(mine, facc_ref[...], 0.0)):
         flux_rows = flux_rows + nn(f, fold)
     flux_row = jnp.sum(flux_rows, axis=0, keepdims=True)
@@ -615,7 +640,7 @@
     def features_back(i, carry):
         cols = pl.ds(pl.multiple_of(i * wide, wide), wide)
         for h in range(2):
-            tt_ref[h, :, cols] = nn(wct_ref[h], v_ref[h, :, cols])
+            tt_ref[h, :, cols] = nn(wct_ref[:, group_part(h)], v_ref[group_part(h), cols])
         return carry
 
     lax.fori_loop(0, side // wide, features_back, 0)
@@ -645,6 +670,7 @@
             total = total + slots[n]
         return total
 
+    hear(2)
     finish(0, p1_ref, corner_peer)
     q1_ref[...] = summed(p1_ref)
     p2_ref[z_at] = q1_ref[...]
@@ -659,11 +685,12 @@
             right = jnp.where(lane == 0, 0.0, pltpu.roll(tt_ref[h, s + 32 : s + 48, :], 1, axis=1))
             parts.append(left + tt_ref[h, s + 16 : s + 32, :] + right)
         tot_ref[c, 0:8, :] = parts[1][0:8]
-        tot_ref[c, 8:12, :] = jnp.zeros((4, side), F32)
-        tot_ref[c, 12:20, :] = parts[1][8:16]
-        tot_ref[c, 4:20, :] += parts[0]
+        tot_ref[c, 8:14, :] = jnp.zeros((6, side), F32)
+        tot_ref[c, 14:22, :] = parts[1][8:16]
+        tot_ref[c, 2:18, :] += parts[0]
         rim_s[0, c : c + 1, :] = parts[1][0:1]
-        rim_s[1, c : c + 1, :] = parts[1][13:14]
+        rim_s[1, c : c + 1, :] = parts[1][11:12]
+
     exchange_start(1, rim_s, rim_r)
 
     span_in(1, across_ref)
@@ -744,7 +771,7 @@
     )
     args = tuple(pltpu.with_memory_space_constraint(a, pltpu.HBM) for a in args)
     chunk = side // GROUP
-    tall = HALF * HID
+    tall = ROWS * HID
     slab = jax.ShapeDtypeStruct(film.shape, F32)
     block = jax.ShapeDtypeStruct((HID, 2 * HID), F32)
     final, grad, gsum = pl.pallas_call(
@@ -764,25 +791,25 @@
             pltpu.VMEM((2, CIN, side), BF),
             pltpu.VMEM((CIN, 24, side), F32),
             pltpu.VMEM((2, PIECES * 16, side), BF),
-            pltpu.VMEM((2, tall, WIDTH), BF),
-            pltpu.VMEM((2, 96, tall), BF),
+            pltpu.VMEM((tall, WIDTH), BF),
+            pltpu.VMEM((96, tall), BF),
             pltpu.VMEM((WIDTH, WIDTH), BF),
             pltpu.VMEM((WIDTH, WIDTH), BF),
-            pltpu.VMEM((16, tall), BF),
+            pltpu.VMEM((16, 3 * WIDTH), BF),
             pltpu.VMEM((WIDTH, 2 * WIDTH), F32),
-            pltpu.VMEM((2, tall, side), BF),
-            pltpu.VMEM((tall, 2 * WIDTH), F32),
-            pltpu.VMEM((2, tall, side), BF),
-            pltpu.VMEM((2, tall, side), BF),
-            pltpu.VMEM((2, tall, side), BF),
+            pltpu.VMEM((tall, side), BF),
+            pltpu.VMEM((3, WIDTH, 2 * WIDTH), F32),
+            pltpu.VMEM((tall, side), BF),
+            pltpu.VMEM((tall, side), BF),
+            pltpu.VMEM((tall, side), BF),
             pltpu.VMEM((rows, side), F32),
             pltpu.VMEM((rows, side), BF),
             pltpu.VMEM((rows, side), BF),
             pltpu.VMEM((rows, side), BF),
             pltpu.VMEM((rows, side), BF),
-            pltpu.VMEM((2, tall, PIECES * 16), F32),
+            pltpu.VMEM((tall, PIECES * 16), F32),
             pltpu.VMEM((2, WIDTH, WIDTH), F32),
-            pltpu.VMEM((HALF, tall), F32),
+            pltpu.VMEM((ROWS, tall), F32),
             pltpu.VMEM((2, 96, side), F32),
             pltpu.VMEM((2, 24, side), F32),
             pltpu.VMEM((2, 2, side), F32),
@@ -804,6 +831,7 @@
             pltpu.SemaphoreType.DMA((2, 2)),
             pltpu.SemaphoreType.DMA((4,)),
             pltpu.SemaphoreType.DMA((4,)),
+            pltpu.SemaphoreType.REGULAR((3,)),
         ],
         compiler_params=pltpu.CompilerParams(
             collective_id=0, has_side_effects=True, vmem_limit_bytes=48 * 1024 * 1024

time: 47.5 us -> 46.1 us (0.971)
  Pallas kernels: 46.7 us -> 45.3 us
    pallas_call x1, Pallas kernels: 46 us -> 44.5 us  [on_device(): pl.pallas_call(kernel, out_shape=(slab, slab, block), in_specs=[hbm] * 10...]
where the time goes in v5:
time: 46.1 us; the launch traced here: 45.9 us
  Pallas kernels  45.3 us (98%)
  between operations  0.64 us (1%)
    pallas_call x1, Pallas kernels, on_device(): pl.pallas_call(kernel, out_shape=(slab, slab, block), in_specs=[hbm] * 10...  44.5 us

profile of v5, /device:TPU:1, one launch (start us, length us, event | category | flops | bytes accessed | tf_op | source)
XLA Modules:
  0.0 45.9 jit_solution(15209635366118663095)
XLA Ops:
  0.6 44.5 %shard_map.137 = (f32[1,16,2048]{2,1,0:T(8,128)S(1)}, f32[1,16,2048]{2,1,0:T(8,128)S(1)}, f32[64,128]{1,0:T(8,128)S(1)}) custom-call(f32[1,16,2048]{2,1,0:T(8,128)} %film_hbm.1, f32[1,16,2048]{2,1,0:T(8,128)} %evap_hbm.1, s32[1,16,2048]{2,1,0:T(8,128)} %mask_hbm.1, s32[1,16,2048]{2,1,0:T(8,128)} %bitcast.3, s32[1,16,16]{2,1,0:T(8,128)} %scls_hbm.1, ...), custom_call_target="tpu_custom_call" | custom-call | tf_op jit(solution)/shard_map/pallas_call | solution.py:777
  45.2 0.7 %shard_map.138 = (f32[1,16,2048]{2,1,0:T(8,128)}, f32[1,16,2048]{2,1,0:T(8,128)}, f32[3,3,4,64]{3,2,1,0:T(4,128)}, f32[64,64]{1,0:T(8,128)}, f32[1,64]{1,0:T(1,128)}) custom-call(f32[1,16,2048]{2,1,0:T(8,128)S(1)} %get-tuple-element.13.final_in, f32[1,16,2048]{2,1,0:T(8,128)S(1)} %get-tuple-element.14.grad_in, f32[64,128]{1,0:T(8,128)S(1)} %get-tuple-element.15.gsum_in), custom_call_target="tpu_custom_call" | custom-call | tf_op jit(solution)/shard_map/pallas_call | solution.py:840

commit v6 on v5

--- a/solution.py
+++ b/solution.py
@@ -20,6 +20,8 @@
 GROUP = SPAN // ROWS
 DX, DZ, DYLO, DYHI, DCORE = 4, 8, 4, 2, 2
 TIME_STEP = 0.5
+FAR_FIRST = (4, 3, 5, 2, 6, 1, 7)
+FAR_FIRST_CORNER = (6, 2, 1, 3, 5, 7, 4)
 
 
 def nt(a, b):
@@ -169,6 +171,27 @@
     ar_rsem,
     far_sem,
 ):
+    sp = lax.axis_index("sp")
+    rep = lax.axis_index("rep")
+    nsp = DYLO * DZ * DX
+    has_up = sp > 0
+    has_down = sp < nsp - 1
+    barrier = pltpu.get_barrier_semaphore()
+
+    def at(r, s):
+        return {"rep": r, "sp": s}
+
+    def signal(peer):
+        pl.semaphore_signal(barrier, inc=1, device_id=peer, device_id_type=MESH)
+
+    @pl.when(has_up)
+    def _():
+        signal(at(rep, sp - 1))
+
+    @pl.when(has_down)
+    def _():
+        signal(at(rep, sp + 1))
+
     inputs = [
         pltpu.make_async_copy(hbm, ref, in_sem.at[n])
         for n, (hbm, ref) in enumerate(
@@ -189,9 +212,6 @@
     for copy in inputs[:6]:
         copy.start()
     side = film_ref.shape[2]
-    sp = lax.axis_index("sp")
-    rep = lax.axis_index("rep")
-    nsp = DYLO * DZ * DX
     x_at = mod(sp, DX)
     z_at = mod(div(sp, DX), DZ)
     ylo_at = div(sp, DX * DZ)
@@ -201,9 +221,6 @@
     member = mod(sp, GROUP)
     first = sp - member
 
-    def at(r, s):
-        return {"rep": r, "sp": s}
-
     def group_peer(s):
         return at(rep, first + mod(member + s, GROUP))
 
@@ -223,27 +240,12 @@
             sp + (mod(other, DYLO) - ylo_at) * DX * DZ,
         )
 
-    barrier = pltpu.get_barrier_semaphore()
-    def signal(peer):
-        pl.semaphore_signal(barrier, inc=1, device_id=peer, device_id_type=MESH)
-
     peers = [group_peer(s) for s in range(1, GROUP)]
     peers += [corner_peer(s) for s in range(1, 8)]
     beside = [z_peer(1), z_peer(7), y_peer(1), y_peer(7)]
     peers += beside
-    has_up = sp > 0
-    has_down = sp < nsp - 1
     for peer in peers:
         signal(peer)
-
-    @pl.when(has_up)
-    def _():
-        signal(at(rep, sp - 1))
-
-    @pl.when(has_down)
-    def _():
-        signal(at(rep, sp + 1))
-
     for copy in inputs[6:]:
         copy.start()
 
@@ -332,7 +334,7 @@
 
     def span_out(which, field):
         recv_ref[which, own_rows, :] = field[:, columns_of(member)]
-        for s in range(1, GROUP):
+        for s in FAR_FIRST_CORNER:
             remote(
                 field.at[:, columns_of(mod(member + s, GROUP))],
                 recv_ref.at[which, own_rows],
@@ -360,7 +362,7 @@
             solved = product if c == 0 else jnp.where(classes == c, product, solved)
         mid_ref[which] = solved.astype(BF)
         result[:, columns_of(member)] = mid_ref[which, own_rows, :]
-        for s in range(1, GROUP):
+        for s in FAR_FIRST_CORNER:
             remote(
                 mid_ref.at[which, rows_of(mod(member + s, GROUP))],
                 result.at[:, columns_of(member)],
@@ -511,10 +513,10 @@
 
     pairs = side // wide
     build_pieces(0)
-    lax.fori_loop(0, 1, forward(0, 1), 0)
 
     neighbours = jnp.where(has_up, 1, 0) + jnp.where(has_down, 1, 0)
     pl.semaphore_wait(barrier, len(peers) + neighbours)
+    span_out(0, back_ref)
     exchange_start(0, halo_s, halo_r)
 
     def tell(n):
@@ -525,11 +527,10 @@
         pl.semaphore_wait(far_sem.at[n], len(beside))
 
     tell(0)
-    span_out(0, back_ref)
-
-    lax.fori_loop(1, pairs, forward(0, 1), 0)
-
+
+    lax.fori_loop(0, pairs - 1, forward(0, 1), 0)
     span_solve(0, back_ref, sg_ref)
+    lax.fori_loop(pairs - 1, pairs, forward(0, 1), 0)
 
     hear(0)
     tell(1)
@@ -575,9 +576,11 @@
             products.append((m, mixing, taps))
             if m > 0:
                 add_products(*products[m - 1])
-            if m == 1:
-                cots = jnp.concatenate([group_rows(flux_cots, g) for g in range(2)], axis=0)
-                facc_ref[...] += nt(cots.astype(BF), sa_ref[:, cols])
+            active = (sa_ref[of, cols] * rows).astype(F32)
+            part = active[:HID]
+            for r in range(1, 4):
+                part = part + active[r * HID : (r + 1) * HID]
+            facc_ref[...] += part
         add_products(*products[-1])
         return carry
 
@@ -602,13 +605,15 @@
     right = jnp.zeros((HID, 2 * HID), F32)
     for t in split3(taps):
         right = right + nt(pick, jnp.concatenate([low, t], axis=0))
-    tall = ROWS * HID
-    fold = onehot(mod(iota((tall, 2 * HID), 0), HID) + HID == iota((tall, 2 * HID), 1))
-    mine = div(iota((ROWS, tall), 1), HID) == iota((ROWS, tall), 0)
-    flux_rows = jnp.zeros((ROWS, 2 * HID), F32)
-    for f in split3(jnp.where(mine, facc_ref[...], 0.0)):
-        flux_rows = flux_rows + nn(f, fold)
-    flux_row = jnp.sum(flux_rows, axis=0, keepdims=True)
+    flux_all = facc_ref[...]
+    flux_lanes = flux_all[:, :SPAN]
+    for n in range(1, 4):
+        flux_lanes = flux_lanes + flux_all[:, n * SPAN : (n + 1) * SPAN]
+    flux_row = jnp.zeros((1, 2 * HID), F32)
+    ones = jnp.ones((8, SPAN), BF)
+    spare_rows = jnp.zeros((HID, SPAN), BF)
+    for f in split3(flux_lanes):
+        flux_row = flux_row + nt(ones, jnp.concatenate([spare_rows, f], axis=0))[:1]
     right = right + jnp.where(iota((HID, 2 * HID), 0) == 9 * CIN, flux_row, 0.0)
     g_ref[...] = right
     blocks = []
@@ -621,7 +626,7 @@
     own_block = pl.ds(pl.multiple_of(j_at * 8, 8), 8)
     p1_ref[j_at] = g_ref[own_block, :]
     stage1 = []
-    for s in range(1, 8):
+    for s in FAR_FIRST_CORNER:
         other = mod(j_at + s, 8)
         stage1.append(
             remote(
@@ -655,7 +660,7 @@
         ).wait()
 
     def begin(stage, slots, at_index, source, send_peer):
-        for s in range(1, 8):
+        for s in FAR_FIRST_CORNER if stage == 3 else FAR_FIRST:
             remote(
                 source,
                 slots.at[at_index],
@@ -809,7 +814,7 @@
             pltpu.VMEM((rows, side), BF),
             pltpu.VMEM((tall, PIECES * 16), F32),
             pltpu.VMEM((2, WIDTH, WIDTH), F32),
-            pltpu.VMEM((ROWS, tall), F32),
+            pltpu.VMEM((HID, 2 * WIDTH), F32),
             pltpu.VMEM((2, 96, side), F32),
             pltpu.VMEM((2, 24, side), F32),
             pltpu.VMEM((2, 2, side), F32),

time: 46.1 us -> 44.7 us (0.970)
  Pallas kernels: 45.3 us -> 43.9 us
    pallas_call x1, Pallas kernels: 44.5 us -> 43.2 us  [on_device(): pl.pallas_call(kernel, out_shape=(slab, slab, block), in_specs=[hbm] * 10...]
where the time goes in v6:
time: 44.7 us; the launch traced here: 44.6 us
  Pallas kernels  43.9 us (98%)
  between operations  0.64 us (1%)
    pallas_call x1, Pallas kernels, on_device(): pl.pallas_call(kernel, out_shape=(slab, slab, block), in_specs=[hbm] * 10...  43.2 us

profile of v6, /device:TPU:1, one launch (start us, length us, event | category | flops | bytes accessed | tf_op | source)
XLA Modules:
  0.0 44.6 jit_solution(6695701660505664719)
XLA Ops:
  0.6 43.2 %shard_map.137 = (f32[1,16,2048]{2,1,0:T(8,128)S(1)}, f32[1,16,2048]{2,1,0:T(8,128)S(1)}, f32[64,128]{1,0:T(8,128)S(1)}) custom-call(f32[1,16,2048]{2,1,0:T(8,128)} %film_hbm.1, f32[1,16,2048]{2,1,0:T(8,128)} %evap_hbm.1, s32[1,16,2048]{2,1,0:T(8,128)} %mask_hbm.1, s32[1,16,2048]{2,1,0:T(8,128)} %bitcast.3, s32[1,16,16]{2,1,0:T(8,128)} %scls_hbm.1, ...), custom_call_target="tpu_custom_call" | custom-call | tf_op jit(solution)/shard_map/pallas_call | solution.py:782
  43.8 0.7 %shard_map.138 = (f32[1,16,2048]{2,1,0:T(8,128)}, f32[1,16,2048]{2,1,0:T(8,128)}, f32[3,3,4,64]{3,2,1,0:T(4,128)}, f32[64,64]{1,0:T(8,128)}, f32[1,64]{1,0:T(1,128)}) custom-call(f32[1,16,2048]{2,1,0:T(8,128)S(1)} %get-tuple-element.13.final_in, f32[1,16,2048]{2,1,0:T(8,128)S(1)} %get-tuple-element.14.grad_in, f32[64,128]{1,0:T(8,128)S(1)} %get-tuple-element.15.gsum_in), custom_call_target="tpu_custom_call" | custom-call | tf_op jit(solution)/shard_map/pallas_call | solution.py:845

commit v7 on v6

--- a/solution.py
+++ b/solution.py
@@ -529,6 +529,9 @@
     tell(0)
 
     lax.fori_loop(0, pairs - 1, forward(0, 1), 0)
+    cacc_ref[...] = jnp.zeros_like(cacc_ref)
+    macc_ref[...] = jnp.zeros_like(macc_ref)
+    facc_ref[...] = jnp.zeros_like(facc_ref)
     span_solve(0, back_ref, sg_ref)
     lax.fori_loop(pairs - 1, pairs, forward(0, 1), 0)
 
@@ -548,23 +551,21 @@
     span_out(1, src_ref)
     span_in(0, sg_ref)
 
-    cacc_ref[...] = jnp.zeros_like(cacc_ref)
-    macc_ref[...] = jnp.zeros_like(macc_ref)
-    facc_ref[...] = jnp.zeros_like(facc_ref)
-
     def add_products(m, mixing, taps):
         macc_ref[m % 2] += mixing
-        cacc_ref[chunk_rows(m), :] += taps
+        cacc_ref[chunk_rows(m), : PIECES * 16] += taps
+
+    broad = 2 * wide
 
     def backward(i, carry):
-        cols = pl.ds(pl.multiple_of(i * wide, wide), wide)
+        cols = pl.ds(pl.multiple_of(i * broad, broad), broad)
         flux_cots = TIME_STEP * sg_ref[:, cols].astype(F32)
         products = []
         for m in range(4):
             of = chunk_rows(m)
             rows = jnp.concatenate(
                 [
-                    jnp.broadcast_to(flux_cots[n : n + 1], (HID, wide)).astype(BF)
+                    jnp.broadcast_to(flux_cots[n : n + 1], (HID, broad)).astype(BF)
                     for n in ORDER[4 * m : 4 * m + 4]
                 ],
                 axis=0,
@@ -584,17 +585,15 @@
         add_products(*products[-1])
         return carry
 
-    lax.fori_loop(0, side // wide, backward, 0)
+    lax.fori_loop(0, side // broad, backward, 0)
 
     rolled = {}
     for r, n in enumerate(SHIFTS):
         term = cacc_ref[r * HID : (r + 1) * HID]
         rolled[n] = term if n not in rolled else rolled[n] + term
     taps = jnp.zeros((HID, WIDTH), F32)
-    spare = jnp.zeros((HID, WIDTH - PIECES * 16), F32)
     for n, term in rolled.items():
-        whole = jnp.concatenate([term, spare], axis=1)
-        taps = taps + (whole if n == 0 else pltpu.roll(whole, WIDTH - n, axis=1))
+        taps = taps + (term if n == 0 else pltpu.roll(term, WIDTH - n, axis=1))
     k_at = iota((HID, WIDTH), 0)
     col = iota((HID, WIDTH), 1)
     piece = col // 16
@@ -603,16 +602,16 @@
     pick = onehot((k_at == wanted) & (tap_row < 3) & (piece < PIECES))
     low = jnp.zeros((HID, WIDTH), BF)
     right = jnp.zeros((HID, 2 * HID), F32)
-    for t in split3(taps):
+    for t in split2(taps):
         right = right + nt(pick, jnp.concatenate([low, t], axis=0))
     flux_all = facc_ref[...]
     flux_lanes = flux_all[:, :SPAN]
-    for n in range(1, 4):
+    for n in range(1, 8):
         flux_lanes = flux_lanes + flux_all[:, n * SPAN : (n + 1) * SPAN]
     flux_row = jnp.zeros((1, 2 * HID), F32)
     ones = jnp.ones((8, SPAN), BF)
     spare_rows = jnp.zeros((HID, SPAN), BF)
-    for f in split3(flux_lanes):
+    for f in split2(flux_lanes):
         flux_row = flux_row + nt(ones, jnp.concatenate([spare_rows, f], axis=0))[:1]
     right = right + jnp.where(iota((HID, 2 * HID), 0) == 9 * CIN, flux_row, 0.0)
     g_ref[...] = right
@@ -812,9 +811,9 @@
             pltpu.VMEM((rows, side), BF),
             pltpu.VMEM((rows, side), BF),
             pltpu.VMEM((rows, side), BF),
-            pltpu.VMEM((tall, PIECES * 16), F32),
+            pltpu.VMEM((tall, WIDTH), F32),
             pltpu.VMEM((2, WIDTH, WIDTH), F32),
-            pltpu.VMEM((HID, 2 * WIDTH), F32),
+            pltpu.VMEM((HID, 4 * WIDTH), F32),
             pltpu.VMEM((2, 96, side), F32),
             pltpu.VMEM((2, 24, side), F32),
             pltpu.VMEM((2, 2, side), F32),

time: 44.7 us -> 44.2 us (0.989)
  Pallas kernels: 43.9 us -> 43.4 us
    pallas_call x1, Pallas kernels: 43.2 us -> 42.7 us  [on_device(): pl.pallas_call(kernel, out_shape=(slab, slab, block), in_specs=[hbm] * 10...]
where the time goes in v7:
time: 44.2 us; the launch traced here: 44 us
  Pallas kernels  43.4 us (98%)
  between operations  0.64 us (1%)
    pallas_call x1, Pallas kernels, on_device(): pl.pallas_call(kernel, out_shape=(slab, slab, block), in_specs=[hbm] * 10...  42.7 us

profile of v7, /device:TPU:1, one launch (start us, length us, event | category | flops | bytes accessed | tf_op | source)
XLA Modules:
  0.0 44.0 jit_solution(3524219989080845526)
XLA Ops:
  0.6 42.7 %shard_map.137 = (f32[1,16,2048]{2,1,0:T(8,128)S(1)}, f32[1,16,2048]{2,1,0:T(8,128)S(1)}, f32[64,128]{1,0:T(8,128)S(1)}) custom-call(f32[1,16,2048]{2,1,0:T(8,128)} %film_hbm.1, f32[1,16,2048]{2,1,0:T(8,128)} %evap_hbm.1, s32[1,16,2048]{2,1,0:T(8,128)} %mask_hbm.1, s32[1,16,2048]{2,1,0:T(8,128)} %bitcast.3, s32[1,16,16]{2,1,0:T(8,128)} %scls_hbm.1, ...), custom_call_target="tpu_custom_call" | custom-call | tf_op jit(solution)/shard_map/pallas_call | solution.py:781
  43.3 0.7 %shard_map.138 = (f32[1,16,2048]{2,1,0:T(8,128)}, f32[1,16,2048]{2,1,0:T(8,128)}, f32[3,3,4,64]{3,2,1,0:T(4,128)}, f32[64,64]{1,0:T(8,128)}, f32[1,64]{1,0:T(1,128)}) custom-call(f32[1,16,2048]{2,1,0:T(8,128)S(1)} %get-tuple-element.13.final_in, f32[1,16,2048]{2,1,0:T(8,128)S(1)} %get-tuple-element.14.grad_in, f32[64,128]{1,0:T(8,128)S(1)} %get-tuple-element.15.gsum_in), custom_call_target="tpu_custom_call" | custom-call | tf_op jit(solution)/shard_map/pallas_call | solution.py:844
